TPU v7x, 32 devices: a whole 2x2x4 slice. The times are simulated.
32 devices in a mesh: groups: 2 (over y), tok: 16 (over z, x, core).
Axes of the slice: x: 2, y: 2, z: 4, core: 2. Of those that a mesh axis runs over, the one named last changes fastest.
Arguments:
- queries: bfloat16 [2048, 2048], P(('groups', 'tok')), parts along dimension 0, may hold values from -256 to 256, as said below
- fresh_keys: bfloat16 [2048, 2048], P(('groups', 'tok')), parts along dimension 0, may hold values from -6 to 6, as said below
- fresh_values: bfloat16 [2048, 2048], P(('groups', 'tok')), parts along dimension 0, may hold values from -6 to 6
- stale_keys: bfloat16 [2048, 2048], P(('groups', 'tok')), parts along dimension 0, may hold values from -6 to 6
- stale_values: bfloat16 [2048, 2048], P(('groups', 'tok')), parts along dimension 0, may hold values from -6 to 6
- patch_starts: int32 [32], P('groups'), parts along dimension 0, may hold values from 0 to 1023, as said below
- order_starts: int32 [32], P('groups'), parts along dimension 0, may hold values from 0 to 1023, as said below
Outputs:
- attended: bfloat16 [2048, 2048], P(('groups', 'tok')), parts along dimension 0
There are 2 independent parts, one for each index of `groups`. A program takes and returns all parts, laid end to end along the dimension named above; each array names one. Nothing has to cross between parts.
Inputs may be any that keep to these rules, and one draw needn't show every extreme that they name: `patch_starts`: strictly increasing; the first entry is 0. `order_starts`: the entries of patch_starts, each once, in processing order. `queries`: entries are finite. `fresh_keys`: entries are finite.
All inputs are finite; a program needn't handle non-finite values.
Results may differ from a plain program's by a relative error of at most 0.0049.
Values may be sent and summed in bfloat16 or wider, within the bound.
A program may use at most 128 MiB of HBM per device.

v0:
```python
import functools
import math

import jax
import jax.numpy as jnp
from jax import lax
from jax.experimental import pallas as pl
from jax.experimental.pallas import tpu as pltpu
from jax.sharding import PartitionSpec as P

HEADS = 16
HEAD_DIM = 128
MESH = pl.DeviceIdType.MESH


def attention_kernel(
    devices,
    patch_starts,
    order_starts,
    queries,
    fresh_keys,
    stale_keys,
    fresh_values,
    stale_values,
    out_ref,
    q_buf,
    kv_buf,
    p_fresh,
    p_stale,
    o_buf,
    q_rank,
    k_rank,
    send_sems,
    recv_sems,
    own_sem,
    out_send,
    out_recv,
):
    me = lax.axis_index("tok")
    tok_dev = queries.shape[0]
    group_size = devices // HEADS
    slab = tok_dev // group_size
    tokens = devices * tok_dev
    rows = devices * slab
    my_head = me // group_size
    my_member = me % group_size
    barrier = pltpu.get_barrier_semaphore()

    def peer_of(step):
        return lax.rem(me + step, devices)

    def columns(head):
        return pl.ds(pl.multiple_of(head * HEAD_DIM, HEAD_DIM), HEAD_DIM)

    def row_slab(index, size):
        return pl.ds(pl.multiple_of(index * size, size), size)

    def greet(step, carry):
        pl.semaphore_signal(barrier, inc=1, device_id={"tok": peer_of(step)}, device_id_type=MESH)
        return carry

    lax.fori_loop(1, devices, greet, 0)

    sources = (queries, fresh_keys, stale_keys, fresh_values, stale_values)

    def source_view(which, device):
        head, member = device // group_size, device % group_size
        if which == 0:
            return queries.at[row_slab(member, slab), columns(head)]
        return sources[which].at[:, columns(head)]

    def landing(which, device):
        if which == 0:
            return q_buf.at[row_slab(device, slab), :]
        return kv_buf.at[which - 1, row_slab(device, tok_dev), :]

    own = [
        pltpu.make_async_copy(source_view(which, me), landing(which, me), own_sem.at[which])
        for which in range(5)
    ]
    for copy in own:
        copy.start()
    pl.semaphore_wait(barrier, devices - 1)

    for which in range(5):

        def send(step, carry, which=which):
            peer = peer_of(step)
            pltpu.make_async_remote_copy(
                src_ref=source_view(which, peer),
                dst_ref=landing(which, me),
                send_sem=send_sems.at[which],
                recv_sem=recv_sems.at[which],
                device_id={"tok": peer},
                device_id_type=MESH,
            ).start()
            return carry

        lax.fori_loop(1, devices, send, 0)

    patches = patch_starts.shape[0]
    starts = [patch_starts[p] for p in range(patches)]
    orders = [order_starts[p] for p in range(patches)]
    ranks = []
    for p in range(patches):
        rank = jnp.int32(0)
        for i in range(patches):
            rank = rank + jnp.where(orders[i] == starts[p], jnp.int32(i), jnp.int32(0))
        ranks.append(rank)
    jumps = [ranks[0]] + [ranks[p] - ranks[p - 1] for p in range(1, patches)]

    def rank_at(positions):
        total = jnp.zeros(positions.shape, jnp.int32)
        for p in range(patches):
            total = total + jnp.where(positions >= starts[p], jumps[p], 0)
        return total

    k_rank[...] = rank_at(lax.broadcasted_iota(jnp.int32, k_rank.shape, 1))

    def fill_rank(device, carry):
        base = device * tok_dev + my_member * slab
        q_rank[row_slab(device, slab), :] = rank_at(
            base + lax.broadcasted_iota(jnp.int32, (slab, HEAD_DIM), 0)
        )
        return carry

    lax.fori_loop(0, devices, fill_rank, 0)

    def all_of(which):
        size = (devices - 1) * (slab if which == 0 else tok_dev)
        return q_buf.at[0:size, :] if which == 0 else kv_buf.at[which - 1, 0:size, :]

    def arrived(which):
        view = all_of(which)
        pltpu.make_async_copy(view, view, recv_sems.at[which]).wait()
        own[which].wait()

    for which in range(3):
        arrived(which)

    score_scale = 1.0 / math.sqrt(HEAD_DIM)
    block = max(slab, min(rows, (1 << 18) // tokens))
    blocks = rows // block
    dims = (((1,), (1,)), ((), ()))

    def probs_block(i, carry):
        at = row_slab(i, block)
        q = q_buf[at, :]
        fresh = lax.dot_general(q, kv_buf[0], dims, preferred_element_type=jnp.float32)
        stale = lax.dot_general(q, kv_buf[1], dims, preferred_element_type=jnp.float32)
        fresh_ok = k_rank[0:1, :] <= q_rank[at, 0:1]
        scores = jnp.where(fresh_ok, fresh, stale) * score_scale
        top = jnp.max(scores, axis=1, keepdims=True)
        weights = jnp.exp(scores - top)
        total = jnp.sum(weights, axis=1, keepdims=True)
        probs = weights * (1.0 / total)
        p_fresh[at, :] = jnp.where(fresh_ok, probs, 0.0).astype(jnp.bfloat16)
        p_stale[at, :] = jnp.where(fresh_ok, 0.0, probs).astype(jnp.bfloat16)
        return carry

    lax.fori_loop(0, blocks, probs_block, 0)

    for which in range(3, 5):
        arrived(which)

    per_block = block // slab

    def give_back(i):
        def one(j, carry):
            target = i * per_block + j

            @pl.when(target != me)
            def _():
                pltpu.make_async_remote_copy(
                    src_ref=o_buf.at[row_slab(target, slab), :],
                    dst_ref=out_ref.at[row_slab(my_member, slab), columns(my_head)],
                    send_sem=out_send,
                    recv_sem=out_recv,
                    device_id={"tok": target},
                    device_id_type=MESH,
                ).start()

            return carry

        lax.fori_loop(0, per_block, one, 0)

    def attend_block(i, carry):
        at = row_slab(i, block)
        mixed = jnp.dot(p_fresh[at, :], kv_buf[2], preferred_element_type=jnp.float32)
        mixed = mixed + jnp.dot(p_stale[at, :], kv_buf[3], preferred_element_type=jnp.float32)
        o_buf[at, :] = mixed.astype(jnp.bfloat16)
        give_back(i)
        return carry

    lax.fori_loop(0, blocks, attend_block, 0)
    mine = pltpu.make_async_copy(
        o_buf.at[row_slab(me, slab), :],
        out_ref.at[row_slab(my_member, slab), columns(my_head)],
        own_sem.at[0],
    )
    mine.start()
    for which in range(5):
        view = all_of(which)
        pltpu.make_async_copy(view, view, send_sems.at[which]).wait()
    view = o_buf.at[0 : (devices - 1) * slab, :]
    mine.wait()
    pltpu.make_async_copy(view, view, out_send).wait()
    pltpu.make_async_copy(view, view, out_recv).wait()


def shards(queries, fresh_keys, fresh_values, stale_keys, stale_values, patch_starts, order_starts):
    devices = lax.axis_size("tok")
    tok_dev, width = queries.shape
    slab = tok_dev // (devices // HEADS)
    tokens, rows = devices * tok_dev, devices * slab
    anywhere = pl.BlockSpec(memory_space=pl.ANY)
    scalars = pl.BlockSpec(memory_space=pltpu.SMEM)
    return pl.pallas_call(
        functools.partial(attention_kernel, devices),
        out_shape=jax.ShapeDtypeStruct((tok_dev, width), jnp.bfloat16),
        in_specs=[scalars] * 2 + [anywhere] * 5,
        out_specs=anywhere,
        scratch_shapes=[
            pltpu.VMEM((rows, HEAD_DIM), jnp.bfloat16),
            pltpu.VMEM((4, tokens, HEAD_DIM), jnp.bfloat16),
            pltpu.VMEM((rows, tokens), jnp.bfloat16),
            pltpu.VMEM((rows, tokens), jnp.bfloat16),
            pltpu.VMEM((rows, HEAD_DIM), jnp.bfloat16),
            pltpu.VMEM((rows, HEAD_DIM), jnp.int32),
            pltpu.VMEM((8, tokens), jnp.int32),
            pltpu.SemaphoreType.DMA((5,)),
            pltpu.SemaphoreType.DMA((5,)),
            pltpu.SemaphoreType.DMA((5,)),
            pltpu.SemaphoreType.DMA,
            pltpu.SemaphoreType.DMA,
        ],
        compiler_params=pltpu.CompilerParams(
            collective_id=0, has_side_effects=True, vmem_limit_bytes=60 * 1024 * 1024
        ),
    )(
        patch_starts,
        order_starts,
        queries,
        fresh_keys,
        stale_keys,
        fresh_values,
        stale_values,
    )


def rank_table(patch_starts, order_starts):
    patches = patch_starts.shape[0]
    starts = [patch_starts[p] for p in range(patches)]
    orders = [order_starts[p] for p in range(patches)]
    ranks = []
    for p in range(patches):
        rank = jnp.int32(0)
        for i in range(patches):
            rank = rank + jnp.where(orders[i] == starts[p], jnp.int32(i), jnp.int32(0))
        ranks.append(rank)
    jumps = [ranks[0]] + [ranks[p] - ranks[p - 1] for p in range(1, patches)]

    def rank_at(positions):
        total = jnp.zeros(positions.shape, jnp.int32)
        for p in range(patches):
            total = total + jnp.where(positions >= starts[p], jumps[p], 0)
        return total

    return rank_at


def halves_kernel(
    devices,
    patch_starts,
    order_starts,
    queries,
    fresh_keys,
    stale_keys,
    fresh_values,
    stale_values,
    parts_ref,
    shares_ref,
    q_buf,
    kv_buf,
    p_fresh,
    p_stale,
    o_buf,
    s_buf,
    stats_ref,
    shares,
    q_rank,
    k_rank,
    q_send,
    q_recv,
    kv_send,
    kv_recv,
    own_q_sem,
    own_sem,
    own_kv_sem,
    o_send,
    o_recv,
    s_send,
    s_recv,
):
    me = lax.axis_index("tok")
    tok_dev = queries.shape[0]
    half = devices // 2
    held = HEADS // half
    tokens = devices * tok_dev
    keys = half * tok_dev
    side, place = me // half, me % half
    barrier = pltpu.get_barrier_semaphore()

    def peer_of(step):
        return lax.rem(me + step, devices)

    def near_peer(step):
        return side * half + lax.rem(place + step, half)

    def columns(head):
        return pl.ds(pl.multiple_of(head * HEAD_DIM, HEAD_DIM), HEAD_DIM)

    def row_slab(index, size):
        return pl.ds(pl.multiple_of(index * size, size), size)

    def greet(step, carry):
        pl.semaphore_signal(barrier, inc=1, device_id={"tok": peer_of(step)}, device_id_type=MESH)
        return carry

    lax.fori_loop(1, devices, greet, 0)

    sources = (fresh_keys, stale_keys, fresh_values, stale_values)

    def q_source(head, device):
        return queries.at[:, columns(device % half * held + head)]

    def kv_source(head, which, device):
        return sources[which].at[:, columns(device % half * held + head)]

    def q_landing(head, device):
        return q_buf.at[head, row_slab(device, tok_dev), :]

    def kv_landing(head, which, device):
        return kv_buf.at[head, which, row_slab(device % half, tok_dev), :]

    own_q = [
        pltpu.make_async_copy(q_source(head, me), q_landing(head, me), own_q_sem.at[head])
        for head in range(held)
    ]
    for copy in own_q:
        copy.start()
    own_kv = [
        [
            pltpu.make_async_copy(
                kv_source(head, which, me), kv_landing(head, which, me), own_kv_sem.at[head, which]
            )
            for which in range(4)
        ]
        for head in range(held)
    ]
    for group in own_kv:
        for copy in group:
            copy.start()
    pl.semaphore_wait(barrier, devices - 1)

    for head in range(held):

        def send_q(step, carry, head=head):
            peer = peer_of(step)
            pltpu.make_async_remote_copy(
                src_ref=q_source(head, peer),
                dst_ref=q_landing(head, me),
                send_sem=q_send.at[head],
                recv_sem=q_recv.at[head],
                device_id={"tok": peer},
                device_id_type=MESH,
            ).start()
            return carry

        lax.fori_loop(1, devices, send_q, 0)
        for which in range(4):

            def send_kv(step, carry, head=head, which=which):
                peer = near_peer(step)
                pltpu.make_async_remote_copy(
                    src_ref=kv_source(head, which, peer),
                    dst_ref=kv_landing(head, which, me),
                    send_sem=kv_send.at[head, which],
                    recv_sem=kv_recv.at[head, which],
                    device_id={"tok": peer},
                    device_id_type=MESH,
                ).start()
                return carry

            lax.fori_loop(1, half, send_kv, 0)

    rank_at = rank_table(patch_starts, order_starts)
    k_rank[...] = rank_at(keys * side + lax.broadcasted_iota(jnp.int32, k_rank.shape, 1))

    def fill_rank(device, carry):
        q_rank[row_slab(device, tok_dev), :] = rank_at(
            device * tok_dev + lax.broadcasted_iota(jnp.int32, (tok_dev, HEAD_DIM), 0)
        )
        return carry

    lax.fori_loop(0, devices, fill_rank, 0)

    def whole_wait(view, sem):
        pltpu.make_async_copy(view, view, sem).wait()

    def q_all(head):
        return q_buf.at[head, 0 : (devices - 1) * tok_dev, :]

    def kv_all(head, which):
        return kv_buf.at[head, which, 0 : (half - 1) * tok_dev, :]

    def arrived(head, which):
        whole_wait(kv_all(head, which), kv_recv.at[head, which])
        own_kv[head][which].wait()

    score_scale = 1.0 / math.sqrt(HEAD_DIM)
    block = min(tokens, 512)
    blocks = tokens // block
    per_block = block // tok_dev
    dims = (((1,), (1,)), ((), ()))
    owner_tile = 128 // tok_dev

    for head in range(held):
        whole_wait(q_all(head), q_recv.at[head])
        own_q[head].wait()
        arrived(head, 0)
        arrived(head, 1)

        def probs_block(i, carry, head=head):
            at = row_slab(i, block)
            q = q_buf[head, at, :]
            fresh = lax.dot_general(q, kv_buf[head, 0], dims, preferred_element_type=jnp.float32)
            stale = lax.dot_general(q, kv_buf[head, 1], dims, preferred_element_type=jnp.float32)
            fresh_ok = k_rank[0:1, :] <= q_rank[at, 0:1]
            scores = jnp.where(fresh_ok, fresh, stale) * score_scale
            top = jnp.max(scores, axis=1, keepdims=True)
            weights = jnp.exp(scores - top)
            total = jnp.sum(weights, axis=1, keepdims=True)
            probs = weights * (1.0 / total)
            p_fresh[at, :] = jnp.where(fresh_ok, probs, 0.0).astype(jnp.bfloat16)
            p_stale[at, :] = jnp.where(fresh_ok, 0.0, probs).astype(jnp.bfloat16)
            level = jnp.broadcast_to(top + jnp.log(total), (block, 128))
            for tile in range(block // 128):
                turned = jnp.transpose(level[tile * 128 : (tile + 1) * 128, :])
                s_buf[i * (block // 128) + tile, head : head + 1, :] = turned[0:1, :]
            return carry

        lax.fori_loop(0, blocks, probs_block, 0)
        arrived(head, 2)
        arrived(head, 3)

        if head == held - 1:

            def send_stats(step, carry):
                peer = peer_of(step)
                pltpu.make_async_remote_copy(
                    src_ref=s_buf.at[peer // owner_tile],
                    dst_ref=stats_ref.at[me],
                    send_sem=s_send,
                    recv_sem=s_recv,
                    device_id={"tok": peer},
                    device_id_type=MESH,
                ).start()
                return carry

        def attend_block(i, carry, head=head):
            at = row_slab(i, block)
            mixed = jnp.dot(p_fresh[at, :], kv_buf[head, 2], preferred_element_type=jnp.float32)
            mixed = mixed + jnp.dot(
                p_stale[at, :], kv_buf[head, 3], preferred_element_type=jnp.float32
            )
            o_buf[head, at, :] = mixed.astype(jnp.bfloat16)

            def give_back(j, carry):
                target = i * per_block + j

                @pl.when(target != me)
                def _():
                    pltpu.make_async_remote_copy(
                        src_ref=o_buf.at[head, row_slab(target, tok_dev), :],
                        dst_ref=parts_ref.at[side, :, columns(place * held + head)],
                        send_sem=o_send.at[head],
                        recv_sem=o_recv.at[head],
                        device_id={"tok": target},
                        device_id_type=MESH,
                    ).start()

                return carry

            lax.fori_loop(0, per_block, give_back, 0)
            return carry

        if head == held - 1:
            lax.fori_loop(1, devices, send_stats, 0)
        lax.fori_loop(0, blocks, attend_block, 0)

    mine = [
        pltpu.make_async_copy(
            o_buf.at[head, row_slab(me, tok_dev), :],
            parts_ref.at[side, :, columns(place * held + head)],
            own_sem.at[1 + head],
        )
        for head in range(held)
    ]
    mine.append(
        pltpu.make_async_copy(
            s_buf.at[me // owner_tile], stats_ref.at[me], own_sem.at[1 + held]
        )
    )
    for copy in mine:
        copy.start()
    s_all = stats_ref.at[0 : devices - 1]
    whole_wait(s_all, s_recv)
    mine[-1].wait()

    def levels(of_side):
        return jnp.concatenate(
            [
                stats_ref[of_side * half + head // held, head % held : head % held + 1, :]
                for head in range(HEADS)
            ],
            axis=0,
        )

    low, high = levels(0), levels(1)
    share = jnp.concatenate(
        [
            1.0 / (1.0 + jnp.exp(high - low)),
            1.0 / (1.0 + jnp.exp(low - high)),
            jnp.zeros((128 - 2 * HEADS, 128), jnp.float32),
        ],
        axis=0,
    )
    shares[...] = jnp.transpose(share)
    for head in range(held):
        whole_wait(q_all(head), q_send.at[head])
        for which in range(4):
            whole_wait(kv_all(head, which), kv_send.at[head, which])
    for copy in mine[:-1]:
        copy.wait()
    whole_wait(s_all, s_send)
    put_shares = pltpu.make_async_copy(
        shares.at[row_slab(me % owner_tile, tok_dev), :], shares_ref, own_sem.at[0]
    )
    put_shares.start()
    for head in range(held):
        o_all = o_buf.at[head, 0 : (devices - 1) * tok_dev, :]
        whole_wait(o_all, o_send.at[head])
        whole_wait(o_all, o_recv.at[head])
    put_shares.wait()


def merge_kernel(parts_in, shares_in, out_ref, parts, mine, merged, sems, out_sems):
    width = out_ref.shape[1]
    chunks = out_sems.shape[0]
    wide = width // chunks
    spans = [pl.ds(chunk * wide, wide) for chunk in range(chunks)]
    shares_copy = pltpu.make_async_copy(shares_in, mine, sems.at[chunks])
    shares_copy.start()
    copies = [
        pltpu.make_async_copy(parts_in.at[:, :, at], parts.at[:, :, at], sems.at[chunk])
        for chunk, at in enumerate(spans)
    ]
    for copy in copies:
        copy.start()
    shares_copy.wait()
    outs = []
    for chunk, span in enumerate(spans):
        copies[chunk].wait()
        for head in range(chunk * wide // HEAD_DIM, (chunk + 1) * wide // HEAD_DIM):
            at = slice(head * HEAD_DIM, (head + 1) * HEAD_DIM)
            low = parts[0, :, at].astype(jnp.float32) * mine[:, head : head + 1]
            high = parts[1, :, at].astype(jnp.float32) * mine[:, HEADS + head : HEADS + head + 1]
            merged[:, at] = (low + high).astype(jnp.bfloat16)
        out = pltpu.make_async_copy(merged.at[:, span], out_ref.at[:, span], out_sems.at[chunk])
        out.start()
        outs.append(out)
    for out in outs:
        out.wait()


def halves(queries, fresh_keys, fresh_values, stale_keys, stale_values, patch_starts, order_starts):
    devices = lax.axis_size("tok")
    tok_dev, width = queries.shape
    half = devices // 2
    held = HEADS // half
    tokens, keys = devices * tok_dev, half * tok_dev
    anywhere = pl.BlockSpec(memory_space=pl.ANY)
    scalars = pl.BlockSpec(memory_space=pltpu.SMEM)
    dma = pltpu.SemaphoreType.DMA
    parts, shares = pl.pallas_call(
        functools.partial(halves_kernel, devices),
        out_shape=(
            jax.ShapeDtypeStruct((2, tok_dev, width), jnp.bfloat16),
            jax.ShapeDtypeStruct((tok_dev, 128), jnp.float32),
        ),
        in_specs=[scalars] * 2 + [anywhere] * 5,
        out_specs=(anywhere, anywhere),
        scratch_shapes=[
            pltpu.VMEM((held, tokens, HEAD_DIM), jnp.bfloat16),
            pltpu.VMEM((held, 4, keys, HEAD_DIM), jnp.bfloat16),
            pltpu.VMEM((tokens, keys), jnp.bfloat16),
            pltpu.VMEM((tokens, keys), jnp.bfloat16),
            pltpu.VMEM((held, tokens, HEAD_DIM), jnp.bfloat16),
            pltpu.VMEM((tokens // 128, held, 128), jnp.float32),
            pltpu.VMEM((devices, held, 128), jnp.float32),
            pltpu.VMEM((128, 128), jnp.float32),
            pltpu.VMEM((tokens, HEAD_DIM), jnp.int32),
            pltpu.VMEM((8, keys), jnp.int32),
            dma((held,)),
            dma((held,)),
            dma((held, 4)),
            dma((held, 4)),
            dma((held,)),
            dma((2 + held,)),
            dma((held, 4)),
            dma((held,)),
            dma((held,)),
            dma,
            dma,
        ],
        compiler_params=pltpu.CompilerParams(
            collective_id=0, has_side_effects=True, vmem_limit_bytes=60 * 1024 * 1024
        ),
    )(patch_starts, order_starts, queries, fresh_keys, stale_keys, fresh_values, stale_values)
    return pl.pallas_call(
        merge_kernel,
        out_shape=jax.ShapeDtypeStruct((tok_dev, width), jnp.bfloat16),
        in_specs=[anywhere, anywhere],
        out_specs=anywhere,
        scratch_shapes=[
            pltpu.VMEM((2, tok_dev, width), jnp.bfloat16),
            pltpu.VMEM((tok_dev, 128), jnp.float32),
            pltpu.VMEM((tok_dev, width), jnp.bfloat16),
            dma((3,)),
            dma((2,)),
        ],
        compiler_params=pltpu.CompilerParams(vmem_limit_bytes=60 * 1024 * 1024),
    )(parts, shares)


def solution(mesh):
    placed = (P(("groups", "tok"), None),) * 5 + (P("groups"),) * 2
    devices = mesh.shape["tok"]

    def body(*arrays):
        tok_dev = arrays[0].shape[0]
        split = devices % 2 == 0 and HEADS % (devices // 2) == 0
        split = split and 128 % tok_dev == 0 and devices * tok_dev % 512 == 0
        return (halves if split else shards)(*arrays)

    return jax.shard_map(
        body, mesh=mesh, in_specs=placed, out_specs=P(("groups", "tok"), None), check_vma=False
    )
```

profile of v0, /device:TPU:0, one launch (start us, length us, event | category | flops | bytes accessed | tf_op | source)
XLA Modules:
  0.0 38.9 jit_solution(4489406516225208194)
XLA Ops:
  0.0 36.7 %shard_map.73 = (bf16[2,64,2048]{2,1,0:T(8,128)(2,1)}, f32[64,128]{1,0:T(8,128)}) custom-call(s32[16]{0:T(128)} %patch_starts.1, s32[16]{0:T(128)} %order_starts.1, bf16[64,2048]{1,0:T(8,128)(2,1)} %queries.1, bf16[64,2048]{1,0:T(8,128)(2,1)} %fresh_keys.1, bf16[64,2048]{1,0:T(8,128)(2,1)} %stale_keys.1, bf16[64,2048]{1,0:T(8,128)(2,1)} %fresh_values.1, ...), custom_call_target="tpu_custom_call" | custom-call | tf_op jit(solution)/shard_map/pallas_call | solution.py:596
  36.7 2.1 %shard_map.74 = bf16[64,2048]{1,0:T(8,128)(2,1)} custom-call(bf16[2,64,2048]{2,1,0:T(8,128)(2,1)} %get-tuple-element.7.parts_in, f32[64,128]{1,0:T(8,128)} %get-tuple-element.8.shares_in), custom_call_target="tpu_custom_call" | custom-call | tf_op jit(solution)/shard_map/pallas_call | solution.py:631
where the time goes:
time: 39.1 us; the launch traced here: 38.9 us
  Pallas kernels  38.9 us (99%)
    pallas_call x1, Pallas kernels, halves(): pl.pallas_call(functools.partial(halves_kernel, devices), out_shape=(jax....  36.7 us
    pallas_call x1, Pallas kernels, halves(): pl.pallas_call(merge_kernel, out_shape=jax.ShapeDtypeStruct((tok_dev, wid...  2.12 us

commit v1 on v0

--- a/solution.py
+++ b/solution.py
@@ -10,6 +10,8 @@
 
 HEADS = 16
 HEAD_DIM = 128
+LAYER = 4
+ISSUE = ((('Q', 0, False), ('K', 0, False), ('ready', 0, False), ('Q', 0, True), ('V', 0, False), ('Q', 1, False), ('pass', 0, False), ('Q', 1, True), ('K', 1, False), ('V', 1, False)), (), (('pass', 1, False),), (), (), (), ())
 MESH = pl.DeviceIdType.MESH
 
 
@@ -269,6 +271,15 @@
     return rank_at
 
 
+def seat(device, half):
+    shift = jnp.where(device >= half, LAYER, 0)
+    return lax.rem(lax.rem(device, half) + shift, half)
+
+
+def is_inner(device, half):
+    return seat(device, half) >= LAYER
+
+
 def halves_kernel(
     devices,
     patch_starts,
@@ -281,7 +292,8 @@
     parts_ref,
     shares_ref,
     q_buf,
-    kv_buf,
+    k_buf,
+    v_buf,
     p_fresh,
     p_stale,
     o_buf,
@@ -292,15 +304,25 @@
     k_rank,
     q_send,
     q_recv,
-    kv_send,
-    kv_recv,
-    own_q_sem,
+    k_send,
+    k_recv,
+    v_send,
+    v_recv,
     own_sem,
-    own_kv_sem,
     o_send,
     o_recv,
     s_send,
     s_recv,
+    ready,
+    lse,
+    twin_lse,
+    twin_part,
+    edge_part,
+    pass_send,
+    l_send,
+    l_recv,
+    t_send,
+    t_recv,
 ):
     me = lax.axis_index("tok")
     tok_dev = queries.shape[0]
@@ -308,91 +330,130 @@
     held = HEADS // half
     tokens = devices * tok_dev
     keys = half * tok_dev
-    side, place = me // half, me % half
+    side, place = lax.div(me, half), lax.rem(me, half)
+    outer_rows = LAYER * tok_dev
+    my_group = seat(me, half)
+    inner = my_group >= LAYER
+    outer = jnp.logical_not(inner)
+    outward = jnp.where(side == 0, -LAYER, LAYER)
+    twin = me - outward
+    near_outer = jnp.where(side == 0, 0, devices - LAYER)
+    far_outer = devices - LAYER - near_outer
     barrier = pltpu.get_barrier_semaphore()
-
-    def peer_of(step):
-        return lax.rem(me + step, devices)
 
     def near_peer(step):
         return side * half + lax.rem(place + step, half)
 
+    def far_peer(step):
+        return (1 - side) * half + lax.rem(place + step, half)
+
     def columns(head):
         return pl.ds(pl.multiple_of(head * HEAD_DIM, HEAD_DIM), HEAD_DIM)
 
-    def row_slab(index, size):
-        return pl.ds(pl.multiple_of(index * size, size), size)
+    def row_slab(index, size, count=1):
+        return pl.ds(pl.multiple_of(index * size, size), size * count)
+
+    def signal(sem, device):
+        pl.semaphore_signal(sem, inc=1, device_id={"tok": device}, device_id_type=MESH)
 
     def greet(step, carry):
-        pl.semaphore_signal(barrier, inc=1, device_id={"tok": peer_of(step)}, device_id_type=MESH)
+        signal(barrier, near_peer(step))
         return carry
 
-    lax.fori_loop(1, devices, greet, 0)
-
-    sources = (fresh_keys, stale_keys, fresh_values, stale_values)
-
-    def q_source(head, device):
-        return queries.at[:, columns(device % half * held + head)]
-
-    def kv_source(head, which, device):
-        return sources[which].at[:, columns(device % half * held + head)]
-
-    def q_landing(head, device):
-        return q_buf.at[head, row_slab(device, tok_dev), :]
-
-    def kv_landing(head, which, device):
-        return kv_buf.at[head, which, row_slab(device % half, tok_dev), :]
-
-    own_q = [
-        pltpu.make_async_copy(q_source(head, me), q_landing(head, me), own_q_sem.at[head])
+    @pl.when(inner)
+    def _():
+        signal(barrier, twin)
+
+    lax.fori_loop(1, half, greet, 0)
+
+    def send(src, dst, send_sem, recv_sem, device):
+        pltpu.make_async_remote_copy(
+            src_ref=src,
+            dst_ref=dst,
+            send_sem=send_sem,
+            recv_sem=recv_sem,
+            device_id={"tok": device},
+            device_id_type=MESH,
+        ).start()
+
+    sources = {"Q": (queries,), "K": (fresh_keys, stale_keys), "V": (fresh_values, stale_values)}
+    near_sems = {"Q": (q_send, q_recv), "K": (k_send, k_recv), "V": (v_send, v_recv)}
+
+    def landing(kind, head, which):
+        if kind == "Q":
+            return q_buf.at[head, row_slab(me, tok_dev), :]
+        return (k_buf if kind == "K" else v_buf).at[head, which, row_slab(place, tok_dev), :]
+
+    def source(kind, head, which, device):
+        return sources[kind][which].at[:, columns(seat(device, half) * held + head)]
+
+    def share_out(kind, head, far=False):
+        def one(step, carry):
+            peer = far_peer(step) if far else near_peer(step)
+            for which in range(len(sources[kind])):
+                at = (head, which)
+                recv_at = at
+                if kind == "Q" and not far:
+                    passed_on = jnp.logical_and(outer, is_inner(peer, half))
+                    recv_at = (head, passed_on.astype(jnp.int32))
+
+                def go(which=which, at=at, recv_at=recv_at, peer=peer):
+                    send(
+                        source(kind, head, which, peer),
+                        landing(kind, head, which),
+                        near_sems[kind][0].at[at],
+                        near_sems[kind][1].at[recv_at],
+                        peer,
+                    )
+
+                if far:
+                    pl.when(jnp.logical_or(inner, jnp.logical_not(is_inner(peer, half))))(go)
+                else:
+                    go()
+            return carry
+
+        lax.fori_loop(0 if far else 1, half, one, 0)
+
+    def pass_on(head):
+        @pl.when(inner)
+        def _():
+            view = q_buf.at[head, row_slab(near_outer, tok_dev, LAYER), :]
+            pltpu.make_async_copy(view, view, q_recv.at[head, 1]).wait()
+            send(view, view, pass_send.at[head], q_recv.at[head, 0], twin)
+
+    def start_all(steps):
+        for kind, head, far in steps:
+            if kind == "pass":
+                pass_on(head)
+            elif kind == "ready":
+                pl.semaphore_wait(ready, 1)
+
+                @pl.when(inner)
+                def _():
+                    signal(ready, me + outward)
+
+            else:
+                share_out(kind, head, far)
+
+    pl.semaphore_wait(barrier, half - 1 + inner.astype(jnp.int32))
+
+    @pl.when(inner)
+    def _():
+        signal(ready, twin)
+
+    start_all(ISSUE[0])
+
+    own = {}
+    for n, (kind, head, which) in enumerate(
+        (kind, head, which)
         for head in range(held)
-    ]
-    for copy in own_q:
-        copy.start()
-    own_kv = [
-        [
-            pltpu.make_async_copy(
-                kv_source(head, which, me), kv_landing(head, which, me), own_kv_sem.at[head, which]
-            )
-            for which in range(4)
-        ]
-        for head in range(held)
-    ]
-    for group in own_kv:
-        for copy in group:
-            copy.start()
-    pl.semaphore_wait(barrier, devices - 1)
-
-    for head in range(held):
-
-        def send_q(step, carry, head=head):
-            peer = peer_of(step)
-            pltpu.make_async_remote_copy(
-                src_ref=q_source(head, peer),
-                dst_ref=q_landing(head, me),
-                send_sem=q_send.at[head],
-                recv_sem=q_recv.at[head],
-                device_id={"tok": peer},
-                device_id_type=MESH,
-            ).start()
-            return carry
-
-        lax.fori_loop(1, devices, send_q, 0)
-        for which in range(4):
-
-            def send_kv(step, carry, head=head, which=which):
-                peer = near_peer(step)
-                pltpu.make_async_remote_copy(
-                    src_ref=kv_source(head, which, peer),
-                    dst_ref=kv_landing(head, which, me),
-                    send_sem=kv_send.at[head, which],
-                    recv_sem=kv_recv.at[head, which],
-                    device_id={"tok": peer},
-                    device_id_type=MESH,
-                ).start()
-                return carry
-
-            lax.fori_loop(1, half, send_kv, 0)
+        for kind in "QKV"
+        for which in range(len(sources[kind]))
+    ):
+        own[kind, head, which] = pltpu.make_async_copy(
+            source(kind, head, which, me), landing(kind, head, which), own_sem.at[n]
+        )
+        own[kind, head, which].start()
 
     rank_at = rank_table(patch_starts, order_starts)
     k_rank[...] = rank_at(keys * side + lax.broadcasted_iota(jnp.int32, k_rank.shape, 1))
@@ -408,15 +469,28 @@
     def whole_wait(view, sem):
         pltpu.make_async_copy(view, view, sem).wait()
 
-    def q_all(head):
-        return q_buf.at[head, 0 : (devices - 1) * tok_dev, :]
-
-    def kv_all(head, which):
-        return kv_buf.at[head, which, 0 : (half - 1) * tok_dev, :]
-
-    def arrived(head, which):
-        whole_wait(kv_all(head, which), kv_recv.at[head, which])
-        own_kv[head][which].wait()
+    def slabs_of(head, count):
+        return q_buf.at[head, 0 : count * tok_dev, :]
+
+    def all_of(kind, head, which):
+        return (k_buf if kind == "K" else v_buf).at[head, which, 0 : (half - 1) * tok_dev, :]
+
+    def arrived(kind, head):
+        for which in range(len(sources[kind])):
+            if kind == "Q":
+                arriving = devices - 1
+
+                @pl.when(inner)
+                def _():
+                    whole_wait(slabs_of(head, arriving - LAYER), q_recv.at[head, 0])
+
+                @pl.when(outer)
+                def _():
+                    whole_wait(slabs_of(head, arriving), q_recv.at[head, 0])
+
+            else:
+                whole_wait(all_of(kind, head, which), near_sems[kind][1].at[head, which])
+            own[kind, head, which].wait()
 
     score_scale = 1.0 / math.sqrt(HEAD_DIM)
     block = min(tokens, 512)
@@ -424,92 +498,138 @@
     per_block = block // tok_dev
     dims = (((1,), (1,)), ((), ()))
     owner_tile = 128 // tok_dev
+    edge_tiles = outer_rows // 128
+
+    def hand_out(head, target):
+        send(
+            o_buf.at[head, row_slab(target, tok_dev), :],
+            parts_ref.at[side, :, columns(my_group * held + head)],
+            o_send.at[head],
+            o_recv.at[head],
+            target,
+        )
+
+    def join(head):
+        @pl.when(inner)
+        def _():
+            whole_wait(twin_lse.at[head], l_recv.at[head])
+            whole_wait(twin_part.at[head], t_recv.at[head])
+            for tile in range(edge_tiles):
+                mine, theirs = lse[head, near_outer // owner_tile + tile], twin_lse[head, tile]
+                w_mine = jnp.broadcast_to(1.0 / (1.0 + jnp.exp(theirs - mine)), (128, 128))
+                w_theirs = jnp.broadcast_to(1.0 / (1.0 + jnp.exp(mine - theirs)), (128, 128))
+                spot = slice(tile * 128, (tile + 1) * 128)
+                full = edge_part[head, spot, :] * jnp.transpose(w_mine)
+                full = full + twin_part[head, spot, :].astype(jnp.float32) * jnp.transpose(w_theirs)
+                at = pl.ds(pl.multiple_of(near_outer * tok_dev + tile * 128, 128), 128)
+                o_buf[head, at, :] = full.astype(jnp.bfloat16)
+
+            def one(j, carry):
+                hand_out(head, near_outer + j)
+                return carry
+
+            lax.fori_loop(0, LAYER, one, 0)
+
 
     for head in range(held):
-        whole_wait(q_all(head), q_recv.at[head])
-        own_q[head].wait()
-        arrived(head, 0)
-        arrived(head, 1)
+        arrived("K", head)
+        arrived("Q", head)
+        start_all(ISSUE[1 + 3 * head])
 
         def probs_block(i, carry, head=head):
             at = row_slab(i, block)
             q = q_buf[head, at, :]
-            fresh = lax.dot_general(q, kv_buf[head, 0], dims, preferred_element_type=jnp.float32)
-            stale = lax.dot_general(q, kv_buf[head, 1], dims, preferred_element_type=jnp.float32)
+            fresh = lax.dot_general(q, k_buf[head, 0], dims, preferred_element_type=jnp.float32)
+            stale = lax.dot_general(q, k_buf[head, 1], dims, preferred_element_type=jnp.float32)
             fresh_ok = k_rank[0:1, :] <= q_rank[at, 0:1]
             scores = jnp.where(fresh_ok, fresh, stale) * score_scale
             top = jnp.max(scores, axis=1, keepdims=True)
             weights = jnp.exp(scores - top)
             total = jnp.sum(weights, axis=1, keepdims=True)
             probs = weights * (1.0 / total)
-            p_fresh[at, :] = jnp.where(fresh_ok, probs, 0.0).astype(jnp.bfloat16)
-            p_stale[at, :] = jnp.where(fresh_ok, 0.0, probs).astype(jnp.bfloat16)
+            p_fresh[head, at, :] = jnp.where(fresh_ok, probs, 0.0).astype(jnp.bfloat16)
+            p_stale[head, at, :] = jnp.where(fresh_ok, 0.0, probs).astype(jnp.bfloat16)
             level = jnp.broadcast_to(top + jnp.log(total), (block, 128))
             for tile in range(block // 128):
                 turned = jnp.transpose(level[tile * 128 : (tile + 1) * 128, :])
                 s_buf[i * (block // 128) + tile, head : head + 1, :] = turned[0:1, :]
+                lse[head, i * (block // 128) + tile] = turned[0:1, :]
             return carry
 
         lax.fori_loop(0, blocks, probs_block, 0)
-        arrived(head, 2)
-        arrived(head, 3)
+        start_all(ISSUE[2 + 3 * head])
+
+        @pl.when(inner)
+        def _(head=head):
+            src = lse.at[head, pl.ds(far_outer // owner_tile, edge_tiles)]
+            send(src, twin_lse.at[head], l_send.at[head], l_recv.at[head], twin)
+
+        if head > 0:
+            join(head - 1)
 
         if head == held - 1:
 
             def send_stats(step, carry):
-                peer = peer_of(step)
-                pltpu.make_async_remote_copy(
-                    src_ref=s_buf.at[peer // owner_tile],
-                    dst_ref=stats_ref.at[me],
-                    send_sem=s_send,
-                    recv_sem=s_recv,
-                    device_id={"tok": peer},
-                    device_id_type=MESH,
-                ).start()
+                peer = lax.rem(me + step, devices)
+                send(s_buf.at[lax.div(peer, owner_tile)], stats_ref.at[me], s_send, s_recv, peer)
                 return carry
 
-        def attend_block(i, carry, head=head):
+            lax.fori_loop(1, devices, send_stats, 0)
+
+        arrived("V", head)
+        start_all(ISSUE[3 + 3 * head])
+
+        def attend_block(n, carry, head=head):
+            i = lax.rem(n + (1 - side) * (blocks // 2), blocks)
             at = row_slab(i, block)
-            mixed = jnp.dot(p_fresh[at, :], kv_buf[head, 2], preferred_element_type=jnp.float32)
+            mixed = jnp.dot(p_fresh[head, at, :], v_buf[head, 0], preferred_element_type=jnp.float32)
             mixed = mixed + jnp.dot(
-                p_stale[at, :], kv_buf[head, 3], preferred_element_type=jnp.float32
+                p_stale[head, at, :], v_buf[head, 1], preferred_element_type=jnp.float32
             )
             o_buf[head, at, :] = mixed.astype(jnp.bfloat16)
+            near = i == side
+
+            @pl.when(jnp.logical_and(inner, near))
+            def _():
+                begin = jnp.where(side == 0, 0, block - outer_rows)
+                for first in (0, block - outer_rows):
+
+                    @pl.when(begin == first)
+                    def _(first=first):
+                        edge_part[head] = mixed[first : first + outer_rows, :]
+
+            @pl.when(jnp.logical_and(inner, jnp.logical_not(near)))
+            def _():
+                src = o_buf.at[head, row_slab(far_outer, tok_dev, LAYER), :]
+                send(src, twin_part.at[head], t_send.at[head], t_recv.at[head], twin)
 
             def give_back(j, carry):
                 target = i * per_block + j
-
-                @pl.when(target != me)
+                direct = jnp.logical_or(outer, is_inner(target, half))
+
+                @pl.when(jnp.logical_and(target != me, direct))
                 def _():
-                    pltpu.make_async_remote_copy(
-                        src_ref=o_buf.at[head, row_slab(target, tok_dev), :],
-                        dst_ref=parts_ref.at[side, :, columns(place * held + head)],
-                        send_sem=o_send.at[head],
-                        recv_sem=o_recv.at[head],
-                        device_id={"tok": target},
-                        device_id_type=MESH,
-                    ).start()
+                    hand_out(head, target)
 
                 return carry
 
             lax.fori_loop(0, per_block, give_back, 0)
             return carry
 
-        if head == held - 1:
-            lax.fori_loop(1, devices, send_stats, 0)
         lax.fori_loop(0, blocks, attend_block, 0)
 
+    join(held - 1)
     mine = [
         pltpu.make_async_copy(
             o_buf.at[head, row_slab(me, tok_dev), :],
-            parts_ref.at[side, :, columns(place * held + head)],
+            parts_ref.at[side, :, columns(my_group * held + head)],
             own_sem.at[1 + head],
         )
         for head in range(held)
     ]
     mine.append(
         pltpu.make_async_copy(
-            s_buf.at[me // owner_tile], stats_ref.at[me], own_sem.at[1 + held]
+            s_buf.at[lax.div(me, owner_tile)], stats_ref.at[me], own_sem.at[1 + held]
         )
     )
     for copy in mine:
@@ -521,41 +641,75 @@
     def levels(of_side):
         return jnp.concatenate(
             [
-                stats_ref[of_side * half + head // held, head % held : head % held + 1, :]
+                stats_ref[
+                    of_side * half + (head // held + of_side * LAYER) % half,
+                    head % held : head % held + 1,
+                    :,
+                ]
                 for head in range(HEADS)
             ],
             axis=0,
         )
 
     low, high = levels(0), levels(1)
+    joined = lax.broadcasted_iota(jnp.int32, low.shape, 0) >= LAYER * held
+    joined = jnp.logical_and(joined, outer)
+    on_low = (side == 0).astype(jnp.float32)
     share = jnp.concatenate(
         [
-            1.0 / (1.0 + jnp.exp(high - low)),
-            1.0 / (1.0 + jnp.exp(low - high)),
+            jnp.where(joined, on_low, 1.0 / (1.0 + jnp.exp(high - low))),
+            jnp.where(joined, 1.0 - on_low, 1.0 / (1.0 + jnp.exp(low - high))),
             jnp.zeros((128 - 2 * HEADS, 128), jnp.float32),
         ],
         axis=0,
     )
     shares[...] = jnp.transpose(share)
+    put_shares = pltpu.make_async_copy(
+        shares.at[row_slab(lax.rem(me, owner_tile), tok_dev), :], shares_ref, own_sem.at[0]
+    )
+    put_shares.start()
     for head in range(held):
-        whole_wait(q_all(head), q_send.at[head])
-        for which in range(4):
-            whole_wait(kv_all(head, which), kv_send.at[head, which])
+        for kind in "KV":
+            for which in range(2):
+                whole_wait(all_of(kind, head, which), near_sems[kind][0].at[head, which])
+
+        @pl.when(inner)
+        def _(head=head):
+            whole_wait(slabs_of(head, devices - 1), q_send.at[head, 0])
+            whole_wait(slabs_of(head, LAYER), pass_send.at[head])
+            whole_wait(twin_lse.at[head], l_send.at[head])
+            whole_wait(twin_part.at[head], t_send.at[head])
+
+        @pl.when(outer)
+        def _(head=head):
+            whole_wait(slabs_of(head, devices - 1 - LAYER), q_send.at[head, 0])
+
     for copy in mine[:-1]:
         copy.wait()
     whole_wait(s_all, s_send)
-    put_shares = pltpu.make_async_copy(
-        shares.at[row_slab(me % owner_tile, tok_dev), :], shares_ref, own_sem.at[0]
-    )
-    put_shares.start()
     for head in range(held):
-        o_all = o_buf.at[head, 0 : (devices - 1) * tok_dev, :]
-        whole_wait(o_all, o_send.at[head])
-        whole_wait(o_all, o_recv.at[head])
+        most = o_buf.at[head, 0 : (devices - 1) * tok_dev, :]
+        less = o_buf.at[head, 0 : (devices - 1 - LAYER) * tok_dev, :]
+
+        @pl.when(inner)
+        def _(head=head, most=most, less=less):
+            whole_wait(less, o_send.at[head])
+            whole_wait(most, o_recv.at[head])
+
+        @pl.when(outer)
+        def _(head=head, most=most, less=less):
+            whole_wait(most, o_send.at[head])
+            whole_wait(less, o_recv.at[head])
+
     put_shares.wait()
 
 
-def merge_kernel(parts_in, shares_in, out_ref, parts, mine, merged, sems, out_sems):
+def merge_kernel(devices, parts_in, shares_in, out_ref, parts, mine, merged, sems, out_sems):
+    me = lax.axis_index("tok")
+    half = devices // 2
+    outer = jnp.logical_not(is_inner(me, half))
+    side = lax.div(me, half)
+    direct = LAYER * (HEADS // half)
     width = out_ref.shape[1]
     chunks = out_sems.shape[0]
     wide = width // chunks
@@ -574,9 +728,21 @@
         copies[chunk].wait()
         for head in range(chunk * wide // HEAD_DIM, (chunk + 1) * wide // HEAD_DIM):
             at = slice(head * HEAD_DIM, (head + 1) * HEAD_DIM)
-            low = parts[0, :, at].astype(jnp.float32) * mine[:, head : head + 1]
-            high = parts[1, :, at].astype(jnp.float32) * mine[:, HEADS + head : HEADS + head + 1]
-            merged[:, at] = (low + high).astype(jnp.bfloat16)
+
+            def both(at=at, head=head):
+                low = parts[0, :, at].astype(jnp.float32) * mine[:, head : head + 1]
+                high = parts[1, :, at].astype(jnp.float32) * mine[:, HEADS + head : HEADS + head + 1]
+                merged[:, at] = (low + high).astype(jnp.bfloat16)
+
+            if head < direct:
+                both()
+            else:
+                pl.when(jnp.logical_not(outer))(both)
+
+                @pl.when(outer)
+                def _(at=at):
+                    merged[:, at] = parts[side, :, at]
+
         out = pltpu.make_async_copy(merged.at[:, span], out_ref.at[:, span], out_sems.at[chunk])
         out.start()
         outs.append(out)
@@ -603,33 +769,44 @@
         out_specs=(anywhere, anywhere),
         scratch_shapes=[
             pltpu.VMEM((held, tokens, HEAD_DIM), jnp.bfloat16),
-            pltpu.VMEM((held, 4, keys, HEAD_DIM), jnp.bfloat16),
-            pltpu.VMEM((tokens, keys), jnp.bfloat16),
-            pltpu.VMEM((tokens, keys), jnp.bfloat16),
+            pltpu.VMEM((held, 2, keys, HEAD_DIM), jnp.bfloat16),
+            pltpu.VMEM((held, 2, keys, HEAD_DIM), jnp.bfloat16),
+            pltpu.VMEM((held, tokens, keys), jnp.bfloat16),
+            pltpu.VMEM((held, tokens, keys), jnp.bfloat16),
             pltpu.VMEM((held, tokens, HEAD_DIM), jnp.bfloat16),
             pltpu.VMEM((tokens // 128, held, 128), jnp.float32),
             pltpu.VMEM((devices, held, 128), jnp.float32),
             pltpu.VMEM((128, 128), jnp.float32),
             pltpu.VMEM((tokens, HEAD_DIM), jnp.int32),
             pltpu.VMEM((8, keys), jnp.int32),
-            dma((held,)),
-            dma((held,)),
-            dma((held, 4)),
-            dma((held, 4)),
-            dma((held,)),
-            dma((2 + held,)),
-            dma((held, 4)),
+            dma((held, 1)),
+            dma((held, 2)),
+            dma((held, 2)),
+            dma((held, 2)),
+            dma((held, 2)),
+            dma((held, 2)),
+            dma((5 * held,)),
             dma((held,)),
             dma((held,)),
             dma,
             dma,
+            pltpu.SemaphoreType.REGULAR,
+            pltpu.VMEM((held, tokens // 128, 1, 128), jnp.float32),
+            pltpu.VMEM((held, LAYER * tok_dev // 128, 1, 128), jnp.float32),
+            pltpu.VMEM((held, LAYER * tok_dev, HEAD_DIM), jnp.bfloat16),
+            pltpu.VMEM((held, LAYER * tok_dev, HEAD_DIM), jnp.float32),
+            dma((held,)),
+            dma((held,)),
+            dma((held,)),
+            dma((held,)),
+            dma((held,)),
         ],
         compiler_params=pltpu.CompilerParams(
             collective_id=0, has_side_effects=True, vmem_limit_bytes=60 * 1024 * 1024
         ),
     )(patch_starts, order_starts, queries, fresh_keys, stale_keys, fresh_values, stale_values)
     return pl.pallas_call(
-        merge_kernel,
+        functools.partial(merge_kernel, devices),
         out_shape=jax.ShapeDtypeStruct((tok_dev, width), jnp.bfloat16),
         in_specs=[anywhere, anywhere],
         out_specs=anywhere,
@@ -651,6 +828,8 @@
     def body(*arrays):
         tok_dev = arrays[0].shape[0]
         split = devices % 2 == 0 and HEADS % (devices // 2) == 0
+        split = split and devices // 2 == 2 * LAYER and LAYER * tok_dev % 128 == 0
+        split = split and 2 * LAYER * tok_dev == 512
         split = split and 128 % tok_dev == 0 and devices * tok_dev % 512 == 0
         return (halves if split else shards)(*arrays)
 

time: 39.1 us -> 37.4 us (0.957)
  Pallas kernels: 38.9 us -> 37 us
    pallas_call x1, Pallas kernels: 36.7 us -> 35 us  [halves(): pl.pallas_call(functools.partial(halves_kernel, devices), out_shape=(jax....]
where the time goes in v1:
time: 37.4 us; the launch traced here: 37 us
  Pallas kernels  37 us (99%)
    pallas_call x1, Pallas kernels, halves(): pl.pallas_call(functools.partial(halves_kernel, devices), out_shape=(jax....  35 us
    pallas_call x1, Pallas kernels, halves(): pl.pallas_call(functools.partial(merge_kernel, devices), out_shape=jax.Sh...  1.97 us

profile of v1, /device:TPU:0, one launch (start us, length us, event | category | flops | bytes accessed | tf_op | source)
XLA Modules:
  0.0 37.0 jit_solution(17920036454833947500)
XLA Ops:
  0.0 35.0 %shard_map.73 = (bf16[2,64,2048]{2,1,0:T(8,128)(2,1)}, f32[64,128]{1,0:T(8,128)}) custom-call(s32[16]{0:T(128)} %patch_starts.1, s32[16]{0:T(128)} %order_starts.1, bf16[64,2048]{1,0:T(8,128)(2,1)} %queries.1, bf16[64,2048]{1,0:T(8,128)(2,1)} %fresh_keys.1, bf16[64,2048]{1,0:T(8,128)(2,1)} %stale_keys.1, bf16[64,2048]{1,0:T(8,128)(2,1)} %fresh_values.1, ...), custom_call_target="tpu_custom_call" | custom-call | tf_op jit(solution)/shard_map/pallas_call | solution.py:762
  35.0 2.0 %shard_map.74 = bf16[64,2048]{1,0:T(8,128)(2,1)} custom-call(bf16[2,64,2048]{2,1,0:T(8,128)(2,1)} %get-tuple-element.7.parts_in, f32[64,128]{1,0:T(8,128)} %get-tuple-element.8.shares_in), custom_call_target="tpu_custom_call" | custom-call | tf_op jit(solution)/shard_map/pallas_call | solution.py:808

commit v2 on v1

--- a/solution.py
+++ b/solution.py
@@ -282,8 +282,8 @@
 
 def halves_kernel(
     devices,
-    patch_starts,
-    order_starts,
+    starts_in,
+    orders_in,
     queries,
     fresh_keys,
     stale_keys,
@@ -314,6 +314,8 @@
     s_send,
     s_recv,
     ready,
+    layout,
+    layout_sem,
     lse,
     twin_lse,
     twin_part,
@@ -365,6 +367,12 @@
         signal(barrier, twin)
 
     lax.fori_loop(1, half, greet, 0)
+    layout_copies = [
+        pltpu.make_async_copy(whole, layout.at[n], layout_sem.at[n])
+        for n, whole in enumerate((starts_in, orders_in))
+    ]
+    for copy in layout_copies:
+        copy.start()
 
     def send(src, dst, send_sem, recv_sem, device):
         pltpu.make_async_remote_copy(
@@ -455,7 +463,9 @@
         )
         own[kind, head, which].start()
 
-    rank_at = rank_table(patch_starts, order_starts)
+    for copy in layout_copies:
+        copy.wait()
+    rank_at = rank_table(layout.at[0], layout.at[1])
     k_rank[...] = rank_at(keys * side + lax.broadcasted_iota(jnp.int32, k_rank.shape, 1))
 
     def fill_rank(device, carry):
@@ -704,35 +714,23 @@
     put_shares.wait()
 
 
-def merge_kernel(devices, parts_in, shares_in, out_ref, parts, mine, merged, sems, out_sems):
+def merge_kernel(devices, parts, shares, out_ref, merged, out_sems):
     me = lax.axis_index("tok")
     half = devices // 2
     outer = jnp.logical_not(is_inner(me, half))
     side = lax.div(me, half)
     direct = LAYER * (HEADS // half)
-    width = out_ref.shape[1]
     chunks = out_sems.shape[0]
-    wide = width // chunks
-    spans = [pl.ds(chunk * wide, wide) for chunk in range(chunks)]
-    shares_copy = pltpu.make_async_copy(shares_in, mine, sems.at[chunks])
-    shares_copy.start()
-    copies = [
-        pltpu.make_async_copy(parts_in.at[:, :, at], parts.at[:, :, at], sems.at[chunk])
-        for chunk, at in enumerate(spans)
-    ]
-    for copy in copies:
-        copy.start()
-    shares_copy.wait()
+    wide = HEADS // chunks
     outs = []
-    for chunk, span in enumerate(spans):
-        copies[chunk].wait()
-        for head in range(chunk * wide // HEAD_DIM, (chunk + 1) * wide // HEAD_DIM):
+    for chunk in range(chunks):
+        for head in range(chunk * wide, (chunk + 1) * wide):
             at = slice(head * HEAD_DIM, (head + 1) * HEAD_DIM)
 
             def both(at=at, head=head):
-                low = parts[0, :, at].astype(jnp.float32) * mine[:, head : head + 1]
-                high = parts[1, :, at].astype(jnp.float32) * mine[:, HEADS + head : HEADS + head + 1]
-                merged[:, at] = (low + high).astype(jnp.bfloat16)
+                low, high = parts[0, :, at].astype(jnp.float32), parts[1, :, at].astype(jnp.float32)
+                share = shares[:, head : head + 1]
+                merged[:, at] = (high + (low - high) * share).astype(jnp.bfloat16)
 
             if head < direct:
                 both()
@@ -743,6 +741,7 @@
                 def _(at=at):
                     merged[:, at] = parts[side, :, at]
 
+        span = pl.ds(chunk * wide * HEAD_DIM, wide * HEAD_DIM)
         out = pltpu.make_async_copy(merged.at[:, span], out_ref.at[:, span], out_sems.at[chunk])
         out.start()
         outs.append(out)
@@ -750,14 +749,18 @@
         out.wait()
 
 
-def halves(queries, fresh_keys, fresh_values, stale_keys, stale_values, patch_starts, order_starts):
+def halves(*arrays):
+    arrays = [pltpu.with_memory_space_constraint(array, pltpu.HBM) for array in arrays]
+    queries, fresh_keys, fresh_values, stale_keys, stale_values, patch_starts, order_starts = arrays
     devices = lax.axis_size("tok")
     tok_dev, width = queries.shape
     half = devices // 2
     held = HEADS // half
     tokens, keys = devices * tok_dev, half * tok_dev
     anywhere = pl.BlockSpec(memory_space=pl.ANY)
-    scalars = pl.BlockSpec(memory_space=pltpu.SMEM)
+    main_memory = pl.BlockSpec(memory_space=pltpu.HBM)
+    near_memory = pl.BlockSpec(memory_space=pltpu.VMEM)
+    patches = patch_starts.shape[0]
     dma = pltpu.SemaphoreType.DMA
     parts, shares = pl.pallas_call(
         functools.partial(halves_kernel, devices),
@@ -765,7 +768,7 @@
             jax.ShapeDtypeStruct((2, tok_dev, width), jnp.bfloat16),
             jax.ShapeDtypeStruct((tok_dev, 128), jnp.float32),
         ),
-        in_specs=[scalars] * 2 + [anywhere] * 5,
+        in_specs=[main_memory] * 7,
         out_specs=(anywhere, anywhere),
         scratch_shapes=[
             pltpu.VMEM((held, tokens, HEAD_DIM), jnp.bfloat16),
@@ -791,6 +794,8 @@
             dma,
             dma,
             pltpu.SemaphoreType.REGULAR,
+            pltpu.SMEM((2, patches), jnp.int32),
+            dma((2,)),
             pltpu.VMEM((held, tokens // 128, 1, 128), jnp.float32),
             pltpu.VMEM((held, LAYER * tok_dev // 128, 1, 128), jnp.float32),
             pltpu.VMEM((held, LAYER * tok_dev, HEAD_DIM), jnp.bfloat16),
@@ -802,22 +807,16 @@
             dma((held,)),
         ],
         compiler_params=pltpu.CompilerParams(
-            collective_id=0, has_side_effects=True, vmem_limit_bytes=60 * 1024 * 1024
+            collective_id=0, has_side_effects=True, vmem_limit_bytes=32 * 1024 * 1024
         ),
     )(patch_starts, order_starts, queries, fresh_keys, stale_keys, fresh_values, stale_values)
     return pl.pallas_call(
         functools.partial(merge_kernel, devices),
         out_shape=jax.ShapeDtypeStruct((tok_dev, width), jnp.bfloat16),
-        in_specs=[anywhere, anywhere],
-        out_specs=anywhere,
-        scratch_shapes=[
-            pltpu.VMEM((2, tok_dev, width), jnp.bfloat16),
-            pltpu.VMEM((tok_dev, 128), jnp.float32),
-            pltpu.VMEM((tok_dev, width), jnp.bfloat16),
-            dma((3,)),
-            dma((2,)),
-        ],
-        compiler_params=pltpu.CompilerParams(vmem_limit_bytes=60 * 1024 * 1024),
+        in_specs=[near_memory, near_memory],
+        out_specs=main_memory,
+        scratch_shapes=[pltpu.VMEM((tok_dev, width), jnp.bfloat16), dma((2,))],
+        compiler_params=pltpu.CompilerParams(vmem_limit_bytes=16 * 1024 * 1024),
     )(parts, shares)
 
 

time: 37.4 us -> 35.3 us (0.944)
  Pallas kernels: 37 us -> 35 us
    pallas_call x1, Pallas kernels: 1.97 us -> 0.89 us  [halves(): pl.pallas_call(functools.partial(merge_kernel, devices), out_shape=jax.Sh...]
    pallas_call x1, Pallas kernels: 35 us -> 34.1 us  [halves(): pl.pallas_call(functools.partial(halves_kernel, devices), out_shape=(jax....]
where the time goes in v2:
time: 35.3 us; the launch traced here: 35 us
  Pallas kernels  35 us (99%)
    pallas_call x1, Pallas kernels, halves(): pl.pallas_call(functools.partial(halves_kernel, devices), out_shape=(jax....  34.1 us
    pallas_call x1, Pallas kernels, halves(): pl.pallas_call(functools.partial(merge_kernel, devices), out_shape=jax.Sh...  0.89 us

profile of v2, /device:TPU:0, one launch (start us, length us, event | category | flops | bytes accessed | tf_op | source)
XLA Modules:
  0.0 35.0 jit_solution(11327235838326309375)
XLA Ops:
  0.0 34.1 %shard_map.73 = (bf16[2,64,2048]{2,1,0:T(8,128)(2,1)S(1)}, f32[64,128]{1,0:T(8,128)S(1)}) custom-call(s32[16]{0:T(128)} %starts_in.1, s32[16]{0:T(128)} %orders_in.1, bf16[64,2048]{1,0:T(8,128)(2,1)} %queries.1, bf16[64,2048]{1,0:T(8,128)(2,1)} %fresh_keys.1, bf16[64,2048]{1,0:T(8,128)(2,1)} %stale_keys.1, bf16[64,2048]{1,0:T(8,128)(2,1)} %fresh_values.1, ...), custom_call_target="tpu_custom_call" | custom-call | tf_op jit(solution)/shard_map/pallas_call | solution.py:765
  34.1 0.9 %shard_map.74 = bf16[64,2048]{1,0:T(8,128)(2,1)} custom-call(bf16[2,64,2048]{2,1,0:T(8,128)(2,1)S(1)} %get-tuple-element.7.parts, f32[64,128]{1,0:T(8,128)S(1)} %get-tuple-element.8.shares), custom_call_target="tpu_custom_call" | custom-call | tf_op jit(solution)/shard_map/pallas_call | solution.py:813

commit v3 on v2

--- a/solution.py
+++ b/solution.py
@@ -11,7 +11,8 @@
 HEADS = 16
 HEAD_DIM = 128
 LAYER = 4
-ISSUE = ((('Q', 0, False), ('K', 0, False), ('ready', 0, False), ('Q', 0, True), ('V', 0, False), ('Q', 1, False), ('pass', 0, False), ('Q', 1, True), ('K', 1, False), ('V', 1, False)), (), (('pass', 1, False),), (), (), (), ())
+ISSUE = ((('Q', 0, ('cross', 'beside'), None), ('K', 0, ('cross', 'beside'), None), ('ready', 0, (), None), ('Q', 0, ('far',), None), ('V', 0, ('cross', 'beside'), None), ('Q', 1, ('cross',), 'outer'), ('Q', 1, ('beside',), None), ('pass', 0, (), None), ('Q', 1, ('far',), None), ('K', 1, ('cross', 'beside'), None), ('V', 1, ('cross', 'beside'), None)), (('Q', 1, ('cross',), 'inner'),), (('pass', 1, (), None),), (), (), (), ())
+HELD_BACK = (0, 1)
 MESH = pl.DeviceIdType.MESH
 
 
@@ -297,19 +298,14 @@
     p_fresh,
     p_stale,
     o_buf,
-    s_buf,
-    stats_ref,
+    stats,
     shares,
     q_rank,
     k_rank,
-    q_send,
+    sent,
     q_recv,
-    k_send,
     k_recv,
-    v_send,
     v_recv,
-    own_sem,
-    o_send,
     o_recv,
     s_send,
     s_recv,
@@ -320,10 +316,8 @@
     twin_lse,
     twin_part,
     edge_part,
-    pass_send,
     l_send,
     l_recv,
-    t_send,
     t_recv,
 ):
     me = lax.axis_index("tok")
@@ -337,6 +331,8 @@
     my_group = seat(me, half)
     inner = my_group >= LAYER
     outer = jnp.logical_not(inner)
+    plane = lax.div(me, LAYER)
+    other_plane = plane + 1 - 2 * lax.rem(plane, 2)
     outward = jnp.where(side == 0, -LAYER, LAYER)
     twin = me - outward
     near_outer = jnp.where(side == 0, 0, devices - LAYER)
@@ -385,7 +381,11 @@
         ).start()
 
     sources = {"Q": (queries,), "K": (fresh_keys, stale_keys), "V": (fresh_values, stale_values)}
-    near_sems = {"Q": (q_send, q_recv), "K": (k_send, k_recv), "V": (v_send, v_recv)}
+    def landed(kind, head):
+        if kind == "Q":
+            return q_recv.at[head, plane]
+        return (k_recv if kind == "K" else v_recv).at[head]
+
 
     def landing(kind, head, which):
         if kind == "Q":
@@ -393,44 +393,50 @@
         return (k_buf if kind == "K" else v_buf).at[head, which, row_slab(place, tok_dev), :]
 
     def source(kind, head, which, device):
-        return sources[kind][which].at[:, columns(seat(device, half) * held + head)]
-
-    def share_out(kind, head, far=False):
-        def one(step, carry):
-            peer = far_peer(step) if far else near_peer(step)
+        return sources[kind][which].at[:, columns(head * half + seat(device, half))]
+
+    def share_out(kind, head, spread):
+        def go(step, peer):
             for which in range(len(sources[kind])):
-                at = (head, which)
-                recv_at = at
-                if kind == "Q" and not far:
-                    passed_on = jnp.logical_and(outer, is_inner(peer, half))
-                    recv_at = (head, passed_on.astype(jnp.int32))
-
-                def go(which=which, at=at, recv_at=recv_at, peer=peer):
-                    send(
-                        source(kind, head, which, peer),
-                        landing(kind, head, which),
-                        near_sems[kind][0].at[at],
-                        near_sems[kind][1].at[recv_at],
-                        peer,
-                    )
-
-                if far:
-                    pl.when(jnp.logical_or(inner, jnp.logical_not(is_inner(peer, half))))(go)
-                else:
-                    go()
+                send(
+                    source(kind, head, which, peer),
+                    landing(kind, head, which),
+                    sent,
+                    landed(kind, head),
+                    peer,
+                )
+
+        def cross(step, carry):
+            go(step, other_plane * LAYER + lax.rem(me + step, LAYER))
             return carry
 
-        lax.fori_loop(0 if far else 1, half, one, 0)
+        def beside(step, carry):
+            go(step, plane * LAYER + lax.rem(me + step, LAYER))
+            return carry
+
+        def far(step, carry):
+            peer = far_peer(step)
+            pl.when(jnp.logical_or(inner, jnp.logical_not(is_inner(peer, half))))(
+                lambda: go(step, peer)
+            )
+            return carry
+
+        if "cross" in spread:
+            lax.fori_loop(0, LAYER, cross, 0)
+        if "beside" in spread:
+            lax.fori_loop(1, LAYER, beside, 0)
+        if "far" in spread:
+            lax.fori_loop(0, half, far, 0)
 
     def pass_on(head):
         @pl.when(inner)
         def _():
             view = q_buf.at[head, row_slab(near_outer, tok_dev, LAYER), :]
-            pltpu.make_async_copy(view, view, q_recv.at[head, 1]).wait()
-            send(view, view, pass_send.at[head], q_recv.at[head, 0], twin)
+            pltpu.make_async_copy(view, view, q_recv.at[head, other_plane]).wait()
+            send(view, view, sent, q_recv.at[head, other_plane], twin)
 
     def start_all(steps):
-        for kind, head, far in steps:
+        for kind, head, spread, who in steps:
             if kind == "pass":
                 pass_on(head)
             elif kind == "ready":
@@ -440,8 +446,12 @@
                 def _():
                     signal(ready, me + outward)
 
+            elif who is not None:
+                pl.when(inner if who == "inner" else outer)(
+                    lambda kind=kind, head=head, spread=spread: share_out(kind, head, spread)
+                )
             else:
-                share_out(kind, head, far)
+                share_out(kind, head, spread)
 
     pl.semaphore_wait(barrier, half - 1 + inner.astype(jnp.int32))
 
@@ -451,17 +461,12 @@
 
     start_all(ISSUE[0])
 
-    own = {}
-    for n, (kind, head, which) in enumerate(
-        (kind, head, which)
-        for head in range(held)
-        for kind in "QKV"
-        for which in range(len(sources[kind]))
-    ):
-        own[kind, head, which] = pltpu.make_async_copy(
-            source(kind, head, which, me), landing(kind, head, which), own_sem.at[n]
-        )
-        own[kind, head, which].start()
+    for head in range(held):
+        for kind in "QKV":
+            for which in range(len(sources[kind])):
+                pltpu.make_async_copy(
+                    source(kind, head, which, me), landing(kind, head, which), landed(kind, head)
+                ).start()
 
     for copy in layout_copies:
         copy.wait()
@@ -479,42 +484,48 @@
     def whole_wait(view, sem):
         pltpu.make_async_copy(view, view, sem).wait()
 
-    def slabs_of(head, count):
-        return q_buf.at[head, 0 : count * tok_dev, :]
-
-    def all_of(kind, head, which):
-        return (k_buf if kind == "K" else v_buf).at[head, which, 0 : (half - 1) * tok_dev, :]
-
     def arrived(kind, head):
-        for which in range(len(sources[kind])):
-            if kind == "Q":
-                arriving = devices - 1
-
-                @pl.when(inner)
-                def _():
-                    whole_wait(slabs_of(head, arriving - LAYER), q_recv.at[head, 0])
-
-                @pl.when(outer)
-                def _():
-                    whole_wait(slabs_of(head, arriving), q_recv.at[head, 0])
-
-            else:
-                whole_wait(all_of(kind, head, which), near_sems[kind][1].at[head, which])
-            own[kind, head, which].wait()
+        whole_wait((k_buf if kind == "K" else v_buf).at[head], landed(kind, head))
+
+    def asked(head, i):
+        @pl.when(jnp.logical_not(jnp.logical_and(inner, i == other_plane)))
+        def _():
+            whole_wait(q_buf.at[head, row_slab(i, outer_rows), :], q_recv.at[head, i])
 
     score_scale = 1.0 / math.sqrt(HEAD_DIM)
-    block = min(tokens, 512)
-    blocks = tokens // block
-    per_block = block // tok_dev
+    block = outer_rows
     dims = (((1,), (1,)), ((), ()))
     owner_tile = 128 // tok_dev
     edge_tiles = outer_rows // 128
 
+    def plane_order(n):
+        last = devices // LAYER - 1
+        swapped = jnp.where(n >= 2, 5 - n, n)
+        return jnp.where(side == 0, last - swapped, swapped)
+
+    def send_levels(head, i):
+        def one(j, carry):
+            target = i * LAYER + j
+
+            @pl.when(target != me)
+            def _():
+                src = lse.at[head, lax.div(target, owner_tile)]
+                send(src, stats.at[head, me], s_send, s_recv.at[head], target)
+
+            return carry
+
+        lax.fori_loop(0, LAYER, one, 0)
+
+        @pl.when(jnp.logical_and(inner, i * LAYER == far_outer))
+        def _():
+            src = lse.at[head, pl.ds(far_outer // owner_tile, edge_tiles)]
+            send(src, twin_lse.at[head], l_send, l_recv.at[head], twin)
+
     def hand_out(head, target):
         send(
             o_buf.at[head, row_slab(target, tok_dev), :],
-            parts_ref.at[side, :, columns(my_group * held + head)],
-            o_send.at[head],
+            parts_ref.at[side, :, columns(head * half + my_group)],
+            sent,
             o_recv.at[head],
             target,
         )
@@ -543,10 +554,11 @@
 
     for head in range(held):
         arrived("K", head)
-        arrived("Q", head)
         start_all(ISSUE[1 + 3 * head])
 
-        def probs_block(i, carry, head=head):
+        def probs_block(n, carry, head=head):
+            i = plane_order(n)
+            asked(head, i)
             at = row_slab(i, block)
             q = q_buf[head, at, :]
             fresh = lax.dot_general(q, k_buf[head, 0], dims, preferred_element_type=jnp.float32)
@@ -562,59 +574,30 @@
             level = jnp.broadcast_to(top + jnp.log(total), (block, 128))
             for tile in range(block // 128):
                 turned = jnp.transpose(level[tile * 128 : (tile + 1) * 128, :])
-                s_buf[i * (block // 128) + tile, head : head + 1, :] = turned[0:1, :]
                 lse[head, i * (block // 128) + tile] = turned[0:1, :]
+            send_levels(head, i)
             return carry
 
-        lax.fori_loop(0, blocks, probs_block, 0)
-        start_all(ISSUE[2 + 3 * head])
-
-        @pl.when(inner)
-        def _(head=head):
-            src = lse.at[head, pl.ds(far_outer // owner_tile, edge_tiles)]
-            send(src, twin_lse.at[head], l_send.at[head], l_recv.at[head], twin)
-
-        if head > 0:
-            join(head - 1)
-
-        if head == held - 1:
-
-            def send_stats(step, carry):
-                peer = lax.rem(me + step, devices)
-                send(s_buf.at[lax.div(peer, owner_tile)], stats_ref.at[me], s_send, s_recv, peer)
-                return carry
-
-            lax.fori_loop(1, devices, send_stats, 0)
-
-        arrived("V", head)
-        start_all(ISSUE[3 + 3 * head])
-
         def attend_block(n, carry, head=head):
-            i = lax.rem(n + (1 - side) * (blocks // 2), blocks)
-            at = row_slab(i, block)
+            i = plane_order(n)
+            at = row_slab(i, outer_rows)
             mixed = jnp.dot(p_fresh[head, at, :], v_buf[head, 0], preferred_element_type=jnp.float32)
             mixed = mixed + jnp.dot(
                 p_stale[head, at, :], v_buf[head, 1], preferred_element_type=jnp.float32
             )
             o_buf[head, at, :] = mixed.astype(jnp.bfloat16)
-            near = i == side
-
-            @pl.when(jnp.logical_and(inner, near))
+
+            @pl.when(jnp.logical_and(inner, i * LAYER == near_outer))
             def _():
-                begin = jnp.where(side == 0, 0, block - outer_rows)
-                for first in (0, block - outer_rows):
-
-                    @pl.when(begin == first)
-                    def _(first=first):
-                        edge_part[head] = mixed[first : first + outer_rows, :]
-
-            @pl.when(jnp.logical_and(inner, jnp.logical_not(near)))
+                edge_part[head] = mixed
+
+            @pl.when(jnp.logical_and(inner, i * LAYER == far_outer))
             def _():
                 src = o_buf.at[head, row_slab(far_outer, tok_dev, LAYER), :]
-                send(src, twin_part.at[head], t_send.at[head], t_recv.at[head], twin)
+                send(src, twin_part.at[head], sent, t_recv.at[head], twin)
 
             def give_back(j, carry):
-                target = i * per_block + j
+                target = i * LAYER + j
                 direct = jnp.logical_or(outer, is_inner(target, half))
 
                 @pl.when(jnp.logical_and(target != me, direct))
@@ -623,130 +606,117 @@
 
                 return carry
 
-            lax.fori_loop(0, per_block, give_back, 0)
+            lax.fori_loop(0, LAYER, give_back, 0)
             return carry
 
-        lax.fori_loop(0, blocks, attend_block, 0)
+        if head > 0:
+            join(head - 1)
+        planes = devices // LAYER
+        early = planes - HELD_BACK[head]
+        lax.fori_loop(0, early, probs_block, 0)
+        start_all(ISSUE[2 + 3 * head])
+        arrived("V", head)
+        start_all(ISSUE[3 + 3 * head])
+        lax.fori_loop(0, early, attend_block, 0)
+        if early < planes:
+            lax.fori_loop(early, planes, probs_block, 0)
+            lax.fori_loop(early, planes, attend_block, 0)
 
     join(held - 1)
-    mine = [
+    for head in range(held):
         pltpu.make_async_copy(
             o_buf.at[head, row_slab(me, tok_dev), :],
-            parts_ref.at[side, :, columns(my_group * held + head)],
-            own_sem.at[1 + head],
-        )
-        for head in range(held)
-    ]
-    mine.append(
+            parts_ref.at[side, :, columns(head * half + my_group)],
+            o_recv.at[head],
+        ).start()
         pltpu.make_async_copy(
-            s_buf.at[lax.div(me, owner_tile)], stats_ref.at[me], own_sem.at[1 + held]
-        )
+            lse.at[head, lax.div(me, owner_tile)], stats.at[head, me], s_recv.at[head]
+        ).start()
+
+    def outputs_in(head):
+        @pl.when(inner)
+        def _():
+            whole_wait(o_buf.at[head], o_recv.at[head])
+
+        @pl.when(outer)
+        def _():
+            whole_wait(o_buf.at[head, 0 : (devices - LAYER) * tok_dev, :], o_recv.at[head])
+
+    for head in range(held):
+        whole_wait(stats.at[head], s_recv.at[head])
+
+        def levels(of_side, head=head):
+            return jnp.concatenate(
+                [
+                    stats[head, of_side * half + (group + of_side * LAYER) % half]
+                    for group in range(half)
+                ],
+                axis=0,
+            )
+
+        share = 1.0 / (1.0 + jnp.exp(levels(1) - levels(0)))
+        share = jnp.concatenate([share, jnp.zeros((128 - half, 128), jnp.float32)], axis=0)
+        shares[...] = jnp.transpose(share)
+        rows = row_slab(lax.rem(me, owner_tile), tok_dev)
+        if head < held - 1:
+            outputs_in(head)
+            merge_slot(head, half, parts_ref, shares.at[rows, :], outer, side, parts_ref.at[0])
+        else:
+            shares_ref[...] = shares[rows, :]
+
+    outputs_in(held - 1)
+    whole_wait(stats.at[:, 0 : devices - 1], s_send)
+    slab = tok_dev * HEAD_DIM
+
+    def all_sent(slabs):
+        whole_wait(p_fresh.at[:, 0 : slabs * slab // keys, :], sent)
+
+    kv, out = 4 * (half - 1), devices - 1
+
+    @pl.when(inner)
+    def _():
+        whole_wait(twin_lse, l_send)
+        all_sent(kv + devices - 1 + LAYER + out)
+
+    @pl.when(outer)
+    def _():
+        all_sent(kv + devices - 1 - LAYER + out)
+
+
+def merge_slot(slot, half, parts, shares, outer, side, out):
+    for head in range(slot * half, (slot + 1) * half):
+        at = slice(head * HEAD_DIM, (head + 1) * HEAD_DIM)
+
+        def both(at=at, head=head):
+            low, high = parts[0, :, at].astype(jnp.float32), parts[1, :, at].astype(jnp.float32)
+            share = shares[:, head % half : head % half + 1]
+            out[:, at] = (high + (low - high) * share).astype(jnp.bfloat16)
+
+        if head % half < LAYER:
+            both()
+        else:
+            pl.when(jnp.logical_not(outer))(both)
+
+            @pl.when(outer)
+            def _(at=at):
+                out[:, at] = parts[side, :, at]
+
+
+def merge_kernel(devices, parts, shares, out_ref, merged, out_sems):
+    half = devices // 2
+    me = lax.axis_index("tok")
+    last = HEADS // half - 1
+    done = last * half * HEAD_DIM
+    early = pltpu.make_async_copy(
+        parts.at[0, :, 0:done], out_ref.at[:, 0:done], out_sems.at[0]
     )
-    for copy in mine:
-        copy.start()
-    s_all = stats_ref.at[0 : devices - 1]
-    whole_wait(s_all, s_recv)
-    mine[-1].wait()
-
-    def levels(of_side):
-        return jnp.concatenate(
-            [
-                stats_ref[
-                    of_side * half + (head // held + of_side * LAYER) % half,
-                    head % held : head % held + 1,
-                    :,
-                ]
-                for head in range(HEADS)
-            ],
-            axis=0,
-        )
-
-    low, high = levels(0), levels(1)
-    joined = lax.broadcasted_iota(jnp.int32, low.shape, 0) >= LAYER * held
-    joined = jnp.logical_and(joined, outer)
-    on_low = (side == 0).astype(jnp.float32)
-    share = jnp.concatenate(
-        [
-            jnp.where(joined, on_low, 1.0 / (1.0 + jnp.exp(high - low))),
-            jnp.where(joined, 1.0 - on_low, 1.0 / (1.0 + jnp.exp(low - high))),
-            jnp.zeros((128 - 2 * HEADS, 128), jnp.float32),
-        ],
-        axis=0,
-    )
-    shares[...] = jnp.transpose(share)
-    put_shares = pltpu.make_async_copy(
-        shares.at[row_slab(lax.rem(me, owner_tile), tok_dev), :], shares_ref, own_sem.at[0]
-    )
-    put_shares.start()
-    for head in range(held):
-        for kind in "KV":
-            for which in range(2):
-                whole_wait(all_of(kind, head, which), near_sems[kind][0].at[head, which])
-
-        @pl.when(inner)
-        def _(head=head):
-            whole_wait(slabs_of(head, devices - 1), q_send.at[head, 0])
-            whole_wait(slabs_of(head, LAYER), pass_send.at[head])
-            whole_wait(twin_lse.at[head], l_send.at[head])
-            whole_wait(twin_part.at[head], t_send.at[head])
-
-        @pl.when(outer)
-        def _(head=head):
-            whole_wait(slabs_of(head, devices - 1 - LAYER), q_send.at[head, 0])
-
-    for copy in mine[:-1]:
-        copy.wait()
-    whole_wait(s_all, s_send)
-    for head in range(held):
-        most = o_buf.at[head, 0 : (devices - 1) * tok_dev, :]
-        less = o_buf.at[head, 0 : (devices - 1 - LAYER) * tok_dev, :]
-
-        @pl.when(inner)
-        def _(head=head, most=most, less=less):
-            whole_wait(less, o_send.at[head])
-            whole_wait(most, o_recv.at[head])
-
-        @pl.when(outer)
-        def _(head=head, most=most, less=less):
-            whole_wait(most, o_send.at[head])
-            whole_wait(less, o_recv.at[head])
-
-    put_shares.wait()
-
-
-def merge_kernel(devices, parts, shares, out_ref, merged, out_sems):
-    me = lax.axis_index("tok")
-    half = devices // 2
+    early.start()
     outer = jnp.logical_not(is_inner(me, half))
-    side = lax.div(me, half)
-    direct = LAYER * (HEADS // half)
-    chunks = out_sems.shape[0]
-    wide = HEADS // chunks
-    outs = []
-    for chunk in range(chunks):
-        for head in range(chunk * wide, (chunk + 1) * wide):
-            at = slice(head * HEAD_DIM, (head + 1) * HEAD_DIM)
-
-            def both(at=at, head=head):
-                low, high = parts[0, :, at].astype(jnp.float32), parts[1, :, at].astype(jnp.float32)
-                share = shares[:, head : head + 1]
-                merged[:, at] = (high + (low - high) * share).astype(jnp.bfloat16)
-
-            if head < direct:
-                both()
-            else:
-                pl.when(jnp.logical_not(outer))(both)
-
-                @pl.when(outer)
-                def _(at=at):
-                    merged[:, at] = parts[side, :, at]
-
-        span = pl.ds(chunk * wide * HEAD_DIM, wide * HEAD_DIM)
-        out = pltpu.make_async_copy(merged.at[:, span], out_ref.at[:, span], out_sems.at[chunk])
-        out.start()
-        outs.append(out)
-    for out in outs:
-        out.wait()
+    merge_slot(last, half, parts, shares, outer, lax.div(me, half), merged)
+    late = pltpu.make_async_copy(merged.at[:, done:], out_ref.at[:, done:], out_sems.at[1])
+    late.start()
+    early.wait()
+    late.wait()
 
 
 def halves(*arrays):
@@ -769,7 +739,7 @@
             jax.ShapeDtypeStruct((tok_dev, 128), jnp.float32),
         ),
         in_specs=[main_memory] * 7,
-        out_specs=(anywhere, anywhere),
+        out_specs=(near_memory, near_memory),
         scratch_shapes=[
             pltpu.VMEM((held, tokens, HEAD_DIM), jnp.bfloat16),
             pltpu.VMEM((held, 2, keys, HEAD_DIM), jnp.bfloat16),
@@ -777,22 +747,17 @@
             pltpu.VMEM((held, tokens, keys), jnp.bfloat16),
             pltpu.VMEM((held, tokens, keys), jnp.bfloat16),
             pltpu.VMEM((held, tokens, HEAD_DIM), jnp.bfloat16),
-            pltpu.VMEM((tokens // 128, held, 128), jnp.float32),
-            pltpu.VMEM((devices, held, 128), jnp.float32),
+            pltpu.VMEM((held, devices, 1, 128), jnp.float32),
             pltpu.VMEM((128, 128), jnp.float32),
             pltpu.VMEM((tokens, HEAD_DIM), jnp.int32),
             pltpu.VMEM((8, keys), jnp.int32),
-            dma((held, 1)),
-            dma((held, 2)),
-            dma((held, 2)),
-            dma((held, 2)),
-            dma((held, 2)),
-            dma((held, 2)),
-            dma((5 * held,)),
+            dma,
+            dma((held, devices // LAYER)),
+            dma((held,)),
             dma((held,)),
             dma((held,)),
             dma,
-            dma,
+            dma((held,)),
             pltpu.SemaphoreType.REGULAR,
             pltpu.SMEM((2, patches), jnp.int32),
             dma((2,)),
@@ -800,9 +765,7 @@
             pltpu.VMEM((held, LAYER * tok_dev // 128, 1, 128), jnp.float32),
             pltpu.VMEM((held, LAYER * tok_dev, HEAD_DIM), jnp.bfloat16),
             pltpu.VMEM((held, LAYER * tok_dev, HEAD_DIM), jnp.float32),
-            dma((held,)),
-            dma((held,)),
-            dma((held,)),
+            dma,
             dma((held,)),
             dma((held,)),
         ],

time: 35.3 us -> 34.5 us (0.977)
  Pallas kernels: 35 us -> 34.3 us
    pallas_call x1, Pallas kernels: 34.1 us -> 33.5 us  [halves(): pl.pallas_call(functools.partial(halves_kernel, devices), out_shape=(jax....]
where the time goes in v3:
time: 34.5 us; the launch traced here: 34.3 us
  Pallas kernels  34.3 us (99%)
    pallas_call x1, Pallas kernels, halves(): pl.pallas_call(functools.partial(halves_kernel, devices), out_shape=(jax....  33.5 us
    pallas_call x1, Pallas kernels, halves(): pl.pallas_call(functools.partial(merge_kernel, devices), out_shape=jax.Sh...  0.81 us

profile of v3, /device:TPU:0, one launch (start us, length us, event | category | flops | bytes accessed | tf_op | source)
XLA Modules:
  0.0 34.3 jit_solution(619127967193003193)
XLA Ops:
  0.0 33.5 %shard_map.73 = (bf16[2,64,2048]{2,1,0:T(8,128)(2,1)S(1)}, f32[64,128]{1,0:T(8,128)S(1)}) custom-call(s32[16]{0:T(128)} %starts_in.1, s32[16]{0:T(128)} %orders_in.1, bf16[64,2048]{1,0:T(8,128)(2,1)} %queries.1, bf16[64,2048]{1,0:T(8,128)(2,1)} %fresh_keys.1, bf16[64,2048]{1,0:T(8,128)(2,1)} %stale_keys.1, bf16[64,2048]{1,0:T(8,128)(2,1)} %fresh_values.1, ...), custom_call_target="tpu_custom_call" | custom-call | tf_op jit(solution)/shard_map/pallas_call | solution.py:735
  33.5 0.8 %shard_map.74 = bf16[64,2048]{1,0:T(8,128)(2,1)} custom-call(bf16[2,64,2048]{2,1,0:T(8,128)(2,1)S(1)} %get-tuple-element.7.parts, f32[64,128]{1,0:T(8,128)S(1)} %get-tuple-element.8.shares), custom_call_target="tpu_custom_call" | custom-call | tf_op jit(solution)/shard_map/pallas_call | solution.py:776

commit v4 on v3

--- a/solution.py
+++ b/solution.py
@@ -609,8 +609,6 @@
             lax.fori_loop(0, LAYER, give_back, 0)
             return carry
 
-        if head > 0:
-            join(head - 1)
         planes = devices // LAYER
         early = planes - HELD_BACK[head]
         lax.fori_loop(0, early, probs_block, 0)
@@ -618,6 +616,8 @@
         arrived("V", head)
         start_all(ISSUE[3 + 3 * head])
         lax.fori_loop(0, early, attend_block, 0)
+        if head > 0:
+            join(head - 1)
         if early < planes:
             lax.fori_loop(early, planes, probs_block, 0)
             lax.fori_loop(early, planes, attend_block, 0)

time: 34.5 us -> 34 us (0.986)
  Pallas kernels: 34.3 us -> 33.6 us
    pallas_call x1, Pallas kernels: 33.5 us -> 32.8 us  [halves(): pl.pallas_call(functools.partial(halves_kernel, devices), out_shape=(jax....]
where the time goes in v4:
time: 34 us; the launch traced here: 33.6 us
  Pallas kernels  33.6 us (99%)
    pallas_call x1, Pallas kernels, halves(): pl.pallas_call(functools.partial(halves_kernel, devices), out_shape=(jax....  32.8 us
    pallas_call x1, Pallas kernels, halves(): pl.pallas_call(functools.partial(merge_kernel, devices), out_shape=jax.Sh...  0.81 us

profile of v4, /device:TPU:0, one launch (start us, length us, event | category | flops | bytes accessed | tf_op | source)
XLA Modules:
  0.0 33.6 jit_solution(14766609474461085607)
XLA Ops:
  0.0 32.8 %shard_map.73 = (bf16[2,64,2048]{2,1,0:T(8,128)(2,1)S(1)}, f32[64,128]{1,0:T(8,128)S(1)}) custom-call(s32[16]{0:T(128)} %starts_in.1, s32[16]{0:T(128)} %orders_in.1, bf16[64,2048]{1,0:T(8,128)(2,1)} %queries.1, bf16[64,2048]{1,0:T(8,128)(2,1)} %fresh_keys.1, bf16[64,2048]{1,0:T(8,128)(2,1)} %stale_keys.1, bf16[64,2048]{1,0:T(8,128)(2,1)} %fresh_values.1, ...), custom_call_target="tpu_custom_call" | custom-call | tf_op jit(solution)/shard_map/pallas_call | solution.py:735
  32.8 0.8 %shard_map.74 = bf16[64,2048]{1,0:T(8,128)(2,1)} custom-call(bf16[2,64,2048]{2,1,0:T(8,128)(2,1)S(1)} %get-tuple-element.7.parts, f32[64,128]{1,0:T(8,128)S(1)} %get-tuple-element.8.shares), custom_call_target="tpu_custom_call" | custom-call | tf_op jit(solution)/shard_map/pallas_call | solution.py:776

commit v5 on v4

--- a/solution.py
+++ b/solution.py
@@ -11,7 +11,7 @@
 HEADS = 16
 HEAD_DIM = 128
 LAYER = 4
-ISSUE = ((('Q', 0, ('cross', 'beside'), None), ('K', 0, ('cross', 'beside'), None), ('ready', 0, (), None), ('Q', 0, ('far',), None), ('V', 0, ('cross', 'beside'), None), ('Q', 1, ('cross',), 'outer'), ('Q', 1, ('beside',), None), ('pass', 0, (), None), ('Q', 1, ('far',), None), ('K', 1, ('cross', 'beside'), None), ('V', 1, ('cross', 'beside'), None)), (('Q', 1, ('cross',), 'inner'),), (('pass', 1, (), None),), (), (), (), ())
+ISSUE = ((('Q', 0, ('straight',), None), ('K', 0, ('straight',), None), ('Q', 0, ('beside',), None), ('wide', 0, (), None), ('Q', 0, ('diagonal',), None), ('K', 0, ('diagonal',), None), ('K', 0, ('beside',), None), ('ready', 0, (), None), ('Q', 0, ('far',), None), ('V', 0, ('straight', 'beside', 'diagonal'), None), ('Q', 1, ('straight', 'diagonal'), 'outer'), ('Q', 1, ('beside',), None), ('pass', 0, (), None), ('Q', 1, ('far',), None), ('K', 1, ('straight', 'beside', 'diagonal'), None), ('V', 1, ('straight', 'beside', 'diagonal'), None)), (), (('pass', 1, (), None), ('Q', 1, ('straight', 'diagonal'), 'inner')), (), (), (), ())
 HELD_BACK = (0, 1)
 MESH = pl.DeviceIdType.MESH
 
@@ -310,6 +310,7 @@
     s_send,
     s_recv,
     ready,
+    wide,
     layout,
     layout_sem,
     lse,
@@ -339,8 +340,14 @@
     far_outer = devices - LAYER - near_outer
     barrier = pltpu.get_barrier_semaphore()
 
-    def near_peer(step):
-        return side * half + lax.rem(place + step, half)
+    column = lax.rem(me, LAYER)
+    mirror = me + 2 - LAYER * lax.div(column, 2)
+
+    def straight_peer(step):
+        return other_plane * LAYER + 2 * lax.div(column, 2) + step
+
+    def diagonal_peer(step):
+        return other_plane * LAYER + 2 - 2 * lax.div(column, 2) + step
 
     def far_peer(step):
         return (1 - side) * half + lax.rem(place + step, half)
@@ -354,15 +361,15 @@
     def signal(sem, device):
         pl.semaphore_signal(sem, inc=1, device_id={"tok": device}, device_id_type=MESH)
 
-    def greet(step, carry):
-        signal(barrier, near_peer(step))
-        return carry
 
     @pl.when(inner)
     def _():
         signal(barrier, twin)
 
-    lax.fori_loop(1, half, greet, 0)
+    for step in range(1, LAYER):
+        signal(barrier, plane * LAYER + lax.rem(me + step, LAYER))
+    for step in range(2):
+        signal(barrier, straight_peer(step))
     layout_copies = [
         pltpu.make_async_copy(whole, layout.at[n], layout_sem.at[n])
         for n, whole in enumerate((starts_in, orders_in))
@@ -406,8 +413,12 @@
                     peer,
                 )
 
-        def cross(step, carry):
-            go(step, other_plane * LAYER + lax.rem(me + step, LAYER))
+        def straight(step, carry):
+            go(step, straight_peer(step))
+            return carry
+
+        def diagonal(step, carry):
+            go(step, diagonal_peer(step))
             return carry
 
         def beside(step, carry):
@@ -421,10 +432,12 @@
             )
             return carry
 
-        if "cross" in spread:
-            lax.fori_loop(0, LAYER, cross, 0)
+        if "straight" in spread:
+            lax.fori_loop(0, 2, straight, 0)
         if "beside" in spread:
             lax.fori_loop(1, LAYER, beside, 0)
+        if "diagonal" in spread:
+            lax.fori_loop(0, 2, diagonal, 0)
         if "far" in spread:
             lax.fori_loop(0, half, far, 0)
 
@@ -439,6 +452,13 @@
         for kind, head, spread, who in steps:
             if kind == "pass":
                 pass_on(head)
+            elif kind == "wide":
+                pl.semaphore_wait(wide, 1)
+
+                @pl.when(inner)
+                def _():
+                    signal(ready, twin)
+
             elif kind == "ready":
                 pl.semaphore_wait(ready, 1)
 
@@ -453,11 +473,9 @@
             else:
                 share_out(kind, head, spread)
 
-    pl.semaphore_wait(barrier, half - 1 + inner.astype(jnp.int32))
-
-    @pl.when(inner)
-    def _():
-        signal(ready, twin)
+    pl.semaphore_wait(barrier, LAYER + 1 + inner.astype(jnp.int32))
+
+    signal(wide, mirror)
 
     start_all(ISSUE[0])
 
@@ -705,18 +723,42 @@
 def merge_kernel(devices, parts, shares, out_ref, merged, out_sems):
     half = devices // 2
     me = lax.axis_index("tok")
+    side = lax.div(me, half)
+    inner = is_inner(me, half)
+    outer = jnp.logical_not(inner)
     last = HEADS // half - 1
-    done = last * half * HEAD_DIM
-    early = pltpu.make_async_copy(
-        parts.at[0, :, 0:done], out_ref.at[:, 0:done], out_sems.at[0]
-    )
-    early.start()
-    outer = jnp.logical_not(is_inner(me, half))
-    merge_slot(last, half, parts, shares, outer, lax.div(me, half), merged)
-    late = pltpu.make_async_copy(merged.at[:, done:], out_ref.at[:, done:], out_sems.at[1])
-    late.start()
-    early.wait()
-    late.wait()
+    middle = last * half + LAYER
+    done, joined = last * half * HEAD_DIM, middle * HEAD_DIM
+
+    def put(source, n, begin, end):
+        return pltpu.make_async_copy(
+            source.at[:, begin:end], out_ref.at[:, begin:end], out_sems.at[n]
+        )
+
+    put(parts.at[0], 0, 0, done).start()
+
+    @pl.when(outer)
+    def _():
+        put(parts.at[side], 2, joined, HEADS * HEAD_DIM).start()
+
+    def merge(heads):
+        for head in heads:
+            at = slice(head * HEAD_DIM, (head + 1) * HEAD_DIM)
+            low, high = parts[0, :, at].astype(jnp.float32), parts[1, :, at].astype(jnp.float32)
+            share = shares[:, head % half : head % half + 1]
+            merged[:, at] = (high + (low - high) * share).astype(jnp.bfloat16)
+
+    merge(range(last * half, middle))
+    put(merged, 1, done, joined).start()
+
+    @pl.when(inner)
+    def _():
+        merge(range(middle, HEADS))
+        put(merged, 2, joined, HEADS * HEAD_DIM).start()
+
+    put(parts.at[0], 0, 0, done).wait()
+    put(merged, 1, done, joined).wait()
+    put(merged, 2, joined, HEADS * HEAD_DIM).wait()
 
 
 def halves(*arrays):
@@ -759,6 +801,7 @@
             dma,
             dma((held,)),
             pltpu.SemaphoreType.REGULAR,
+            pltpu.SemaphoreType.REGULAR,
             pltpu.SMEM((2, patches), jnp.int32),
             dma((2,)),
             pltpu.VMEM((held, tokens // 128, 1, 128), jnp.float32),
@@ -778,7 +821,7 @@
         out_shape=jax.ShapeDtypeStruct((tok_dev, width), jnp.bfloat16),
         in_specs=[near_memory, near_memory],
         out_specs=main_memory,
-        scratch_shapes=[pltpu.VMEM((tok_dev, width), jnp.bfloat16), dma((2,))],
+        scratch_shapes=[pltpu.VMEM((tok_dev, width), jnp.bfloat16), dma((3,))],
         compiler_params=pltpu.CompilerParams(vmem_limit_bytes=16 * 1024 * 1024),
     )(parts, shares)
 

time: 34 us -> 33.7 us (level)
  no operation moved by 1% of the time
where the time goes in v5:
time: 33.7 us; the launch traced here: 33.6 us
  Pallas kernels  33.6 us (100%)
    pallas_call x1, Pallas kernels, halves(): pl.pallas_call(functools.partial(halves_kernel, devices), out_shape=(jax....  32.8 us
    pallas_call x1, Pallas kernels, halves(): pl.pallas_call(functools.partial(merge_kernel, devices), out_shape=jax.Sh...  0.77 us

profile of v5, /device:TPU:0, one launch (start us, length us, event | category | flops | bytes accessed | tf_op | source)
XLA Modules:
  0.0 33.6 jit_solution(18398179431325892789)
XLA Ops:
  0.0 32.8 %shard_map.73 = (bf16[2,64,2048]{2,1,0:T(8,128)(2,1)S(1)}, f32[64,128]{1,0:T(8,128)S(1)}) custom-call(s32[16]{0:T(128)} %starts_in.1, s32[16]{0:T(128)} %orders_in.1, bf16[64,2048]{1,0:T(8,128)(2,1)} %queries.1, bf16[64,2048]{1,0:T(8,128)(2,1)} %fresh_keys.1, bf16[64,2048]{1,0:T(8,128)(2,1)} %stale_keys.1, bf16[64,2048]{1,0:T(8,128)(2,1)} %fresh_values.1, ...), custom_call_target="tpu_custom_call" | custom-call | tf_op jit(solution)/shard_map/pallas_call | solution.py:777
  32.8 0.8 %shard_map.74 = bf16[64,2048]{1,0:T(8,128)(2,1)} custom-call(bf16[2,64,2048]{2,1,0:T(8,128)(2,1)S(1)} %get-tuple-element.7.parts, f32[64,128]{1,0:T(8,128)S(1)} %get-tuple-element.8.shares), custom_call_target="tpu_custom_call" | custom-call | tf_op jit(solution)/shard_map/pallas_call | solution.py:819

commit v6 on v5

--- a/solution.py
+++ b/solution.py
@@ -582,14 +582,14 @@
             fresh = lax.dot_general(q, k_buf[head, 0], dims, preferred_element_type=jnp.float32)
             stale = lax.dot_general(q, k_buf[head, 1], dims, preferred_element_type=jnp.float32)
             fresh_ok = k_rank[0:1, :] <= q_rank[at, 0:1]
-            scores = jnp.where(fresh_ok, fresh, stale) * score_scale
+            scores = jnp.where(fresh_ok, fresh, stale)
             top = jnp.max(scores, axis=1, keepdims=True)
-            weights = jnp.exp(scores - top)
+            weights = jnp.exp2((scores - top) * (score_scale * math.log2(math.e)))
             total = jnp.sum(weights, axis=1, keepdims=True)
             probs = weights * (1.0 / total)
             p_fresh[head, at, :] = jnp.where(fresh_ok, probs, 0.0).astype(jnp.bfloat16)
             p_stale[head, at, :] = jnp.where(fresh_ok, 0.0, probs).astype(jnp.bfloat16)
-            level = jnp.broadcast_to(top + jnp.log(total), (block, 128))
+            level = jnp.broadcast_to(top * score_scale + jnp.log(total), (block, 128))
             for tile in range(block // 128):
                 turned = jnp.transpose(level[tile * 128 : (tile + 1) * 128, :])
                 lse[head, i * (block // 128) + tile] = turned[0:1, :]

time: 33.7 us -> 33.7 us (level)
  no operation moved by 1% of the time
where the time goes in v6:
time: 33.7 us; the launch traced here: 33.6 us
  Pallas kernels  33.6 us (100%)
    pallas_call x1, Pallas kernels, halves(): pl.pallas_call(functools.partial(halves_kernel, devices), out_shape=(jax....  32.8 us
    pallas_call x1, Pallas kernels, halves(): pl.pallas_call(functools.partial(merge_kernel, devices), out_shape=jax.Sh...  0.77 us

profile of v6, /device:TPU:0, one launch (start us, length us, event | category | flops | bytes accessed | tf_op | source)
XLA Modules:
  0.0 33.6 jit_solution(18424244317281860481)
XLA Ops:
  0.0 32.8 %shard_map.73 = (bf16[2,64,2048]{2,1,0:T(8,128)(2,1)S(1)}, f32[64,128]{1,0:T(8,128)S(1)}) custom-call(s32[16]{0:T(128)} %starts_in.1, s32[16]{0:T(128)} %orders_in.1, bf16[64,2048]{1,0:T(8,128)(2,1)} %queries.1, bf16[64,2048]{1,0:T(8,128)(2,1)} %fresh_keys.1, bf16[64,2048]{1,0:T(8,128)(2,1)} %stale_keys.1, bf16[64,2048]{1,0:T(8,128)(2,1)} %fresh_values.1, ...), custom_call_target="tpu_custom_call" | custom-call | tf_op jit(solution)/shard_map/pallas_call | solution.py:777
  32.8 0.8 %shard_map.74 = bf16[64,2048]{1,0:T(8,128)(2,1)} custom-call(bf16[2,64,2048]{2,1,0:T(8,128)(2,1)S(1)} %get-tuple-element.7.parts, f32[64,128]{1,0:T(8,128)S(1)} %get-tuple-element.8.shares), custom_call_target="tpu_custom_call" | custom-call | tf_op jit(solution)/shard_map/pallas_call | solution.py:819
